TPU v7x, 256 devices: a whole 4x4x8 slice. The times are simulated.
256 devices in a mesh: seq: 64 (over z, y, core), tp: 4 (over x).
Axes of the slice: x: 4, y: 4, z: 8, core: 2. Of those that a mesh axis runs over, the one named last changes fastest.
Arguments:
- db_tokens: int32 [32768, 128], P('seq'), may hold values from 0 to 16383
- db_parent: int32 [32768, 128], P('seq'), may hold values from 0 to 126, as said below
- db_depth: int32 [32768, 128], P('seq'), may hold values from 0 to 31, as said below
- nb_rows: int32 [512, 2], P('seq'), may hold values from 0 to 32767, as said below
- seq_start: int32 [512], P('seq'), may hold values 0 or 1
- table: bfloat16 [16384, 1024], P(None, 'tp'), may hold values from -40 to 40
- depth_table: bfloat16 [32, 1024], P(None, 'tp'), may hold values from -3 to 3
- enc_gain: float32 [1024], replicated, may hold values from 0.25 to 1.75
- enc_qkv: bfloat16 [1024, 3, 1024], P('seq', None, 'tp'), may hold values from -0.1875 to 0.1875
- tree_bias: float32 [8], replicated, may hold values from 1 to 4
- enc_wo: bfloat16 [1024, 1024], P('tp', 'seq'), may hold values from -0.1875 to 0.1875
- cond_kv: bfloat16 [32768, 2, 1024], P('seq', None, 'tp'), may hold values from -150 to 150
- queries: bfloat16 [32768, 4096], P('seq', 'tp'), may hold values from -150 to 150
- cca_kv: bfloat16 [1024, 2, 512], P('seq', None, 'tp'), may hold values from -0.1875 to 0.1875
Outputs:
- attended: bfloat16 [32768, 4096], P('seq', 'tp')
Inputs may be any that keep to these rules, and one draw needn't show every extreme that they name: `db_parent`: position 0 of every stored neighbour is its own parent; every other position's parent is one of the three positions just before it. `db_depth`: position 0 has depth 0; every other position has its parent's depth plus one, capped at 31. `nb_rows`: rows 512 * i to 512 * (i + 1) - 1 of the database lie on index i of seq. Of the 16 neighbours of one index's blocks at most 1 lie on any one index; at most 32 neighbours of all blocks lie on one index, and in every draw some index holds exactly 32.
All inputs are finite; a program needn't handle non-finite values. No bound on the sum of `seq_start` on one device may be relied on, other than what follows from the above.
Results may differ from a plain program's by a relative error of at most 0.0223.
The roundings to bfloat16 on the way count: a program that leaves them out, or rounds other values in their place, can miss the bound.
Values may be sent and summed in bfloat16 or wider, within the bound.
No kernel may reach another device: no remote copies, remote signals or barrier semaphores. Data moves between devices by JAX's collectives and lax.ppermute only.
A program may use at most 128 MiB of HBM per device.

v0:
```python
import functools
import math

import jax
import jax.numpy as jnp
from jax import lax
from jax.experimental import pallas as pl
from jax.experimental.pallas import tpu as pltpu
from jax.sharding import Mesh, PartitionSpec as P

HD = 128
SHARE = 16
GROUP = 4
SCALE = 1.0 / math.sqrt(HD)


SEQ = ("z", "y", "core")


def exchange(value, axis):
    return lax.all_to_all(value, axis, split_axis=0, concat_axis=0, tiled=True)


def swapped(value, axis, distance):
    count = lax.axis_size(axis)
    return lax.ppermute(value, axis, [(i, i ^ distance) for i in range(count)])


def doubled(value, axis, distance):
    return jnp.concatenate([value, swapped(value, axis, distance)], axis=0)


def assemble(refs, place_ref, target, first, count):
    for r, ref in enumerate(refs):
        slots = ref.shape[0]

        def copy(slot, carry, ref=ref, r=r):
            row = pl.multiple_of(place_ref[r, slot] * SHARE, SHARE)
            for a in range(count):
                target[first + a, pl.ds(row, SHARE), :] = ref[slot, pl.ds(a * SHARE, SHARE), :]
            return carry

        lax.fori_loop(0, slots, copy, 0, unroll=8)


def encoder_body(
    parts, my_units, length, cond_len, place_ref, xs_ref, bias_ref, emb_ref, gain_ref, hit_ref, cond_ref, *refs
):
    wa_refs, wo_refs, wc_refs = refs[:parts], refs[parts : 2 * parts], refs[2 * parts : 3 * parts]
    out_ref, normed_ref, acc_ref, enc_ref, mixed_ref, buf_ref = refs[3 * parts :]
    step = pl.program_id(0)
    pieces, rows, columns = emb_ref.shape
    width = pieces * columns
    nt = (((1,), (1,)), ((), ()))
    nn = (((1,), (0,)), ((), ()))

    @pl.when(step == 0)
    def _():
        for n in range(my_units):
            here = pl.ds(n * length, length)
            value = jnp.concatenate(
                [emb_ref[t, here, :].astype(jnp.float32) for t in range(pieces)], axis=1
            )
            acc_ref[here, :] = value
            mean = jnp.sum(value * value, axis=1, keepdims=True) * (1.0 / width)
            normed_ref[here, :] = (value * lax.rsqrt(mean + 1e-05) * gain_ref[...]).astype(jnp.bfloat16)

    @pl.when(step < pieces)
    def _():
        head = xs_ref[step] * (columns // HD)
        assemble(wa_refs, place_ref, buf_ref, 0, 3)
        assemble(wo_refs, place_ref, buf_ref, 3, 1)
        normed = normed_ref[...]
        project = lambda a: lax.dot_general(
            normed, buf_ref[a], nn, preferred_element_type=jnp.float32
        ).astype(jnp.bfloat16)
        query, key, value = project(0), project(1), project(2)
        hit = hit_ref[...].astype(jnp.float32)
        per_block = rows // (cond_ref.shape[1] // cond_len)
        for h in range(columns // HD):
            cols = slice(h * HD, (h + 1) * HD)
            scores, mixing = [], []
            for n in range(my_units):
                here = slice(n * length, (n + 1) * length)
                cond_rows = pl.ds(n * length // per_block * cond_len, cond_len)
                cond_key = cond_ref[0, cond_rows, pl.ds(h * HD, HD)]
                cond_value = cond_ref[0, cond_rows, pl.ds(columns + h * HD, HD)]
                keys = jnp.concatenate([key[here, cols], cond_key, cond_key], axis=0)
                mixing.append(jnp.concatenate([value[here, cols], cond_value, cond_value], axis=0))
                scores.append(
                    lax.dot_general(query[here, cols], keys, nt, preferred_element_type=jnp.float32)
                )
            scores = jnp.concatenate(scores, axis=0) * SCALE
            self_scores = scores[:, :length] + bias_ref[head + h] * hit
            cond_scores = scores[:, length:]
            top = jnp.max(jnp.maximum(self_scores, cond_scores), axis=1, keepdims=True)
            self_e = jnp.exp(self_scores - top)
            cond_e = 0.5 * jnp.exp(cond_scores - top)
            inverse = 1.0 / jnp.sum(self_e + cond_e, axis=1, keepdims=True)
            weights = jnp.concatenate([self_e * inverse, cond_e * inverse], axis=1).astype(jnp.bfloat16)
            for n in range(my_units):
                here = slice(n * length, (n + 1) * length)
                mixed_ref[here, cols] = lax.dot_general(
                    weights[here], mixing[n], nn, preferred_element_type=jnp.float32
                ).astype(jnp.bfloat16)
        acc_ref[...] += lax.dot_general(
            mixed_ref[...], buf_ref[3], nt, preferred_element_type=jnp.float32
        )

    @pl.when(step == pieces)
    def _():
        enc_ref[...] = acc_ref[...].astype(jnp.bfloat16)

    @pl.when(step >= pieces)
    def _():
        assemble(wc_refs, place_ref, buf_ref, 4, 1)
        out_ref[0] = lax.dot_general(
            enc_ref[...], buf_ref[4], nn, preferred_element_type=jnp.float32
        ).astype(jnp.bfloat16)


def encoder(place, xs, bias, emb, gain, hit, cond, weights, my_units, length, cond_len):
    pieces, rows, columns = emb.shape
    width = pieces * columns
    last = pieces - 1
    full = lambda shape: pl.BlockSpec(shape, lambda i, p, x: (0,) * len(shape))
    specs = {"a": [], "o": [], "c": []}
    arrays = {"a": [], "o": [], "c": []}
    for kind, array, height, index in weights:
        pick = (
            (lambda i: jnp.minimum(i, last)) if kind in "ao" else (lambda i: jnp.maximum(i - pieces, 0))
        )
        specs[kind].append(
            pl.BlockSpec(
                (None, array.shape[1], height, columns),
                lambda i, p, x, pick=pick, index=index: (pick(i), 0, index, 0),
            )
        )
        arrays[kind].append(array)
    parts = len(specs["a"])
    return pl.pallas_call(
        functools.partial(encoder_body, parts, my_units, length, cond_len),
        out_shape=jax.ShapeDtypeStruct((pieces, rows, columns), jnp.bfloat16),
        grid_spec=pltpu.PrefetchScalarGridSpec(
            num_scalar_prefetch=2,
            grid=(2 * pieces,),
            in_specs=[
                pl.BlockSpec(memory_space=pltpu.SMEM),
                full(emb.shape),
                full(gain.shape),
                full(hit.shape),
                pl.BlockSpec(
                    (1,) + cond.shape[1:], lambda i, p, x: (jnp.minimum(i, last), 0, 0)
                ),
                *specs["a"],
                *specs["o"],
                *specs["c"],
            ],
            out_specs=pl.BlockSpec(
                (1, rows, columns), lambda i, p, x: (x[jnp.maximum(i - pieces, 0)], 0, 0)
            ),
            scratch_shapes=[
                pltpu.VMEM((rows, width), jnp.bfloat16),
                pltpu.VMEM((rows, width), jnp.float32),
                pltpu.VMEM((rows, width), jnp.bfloat16),
                pltpu.VMEM((rows, columns), jnp.bfloat16),
                pltpu.VMEM((5, width, columns), jnp.bfloat16),
            ],
        ),
        compiler_params=pltpu.CompilerParams(
            dimension_semantics=("arbitrary",), vmem_limit_bytes=48 * 1024 * 1024
        ),
        name="encoder",
    )(place, xs, bias, emb, gain, hit, cond, *arrays["a"], *arrays["o"], *arrays["c"])


def attend_body(heads, group, allowed_ref, q_ref, cur_ref, prev_ref, carried_ref, out_ref):
    step = pl.program_id(0)
    nt = (((1,), (1,)), ((), ()))
    nn = (((1,), (0,)), ((), ()))
    tokens = q_ref.shape[0] // group
    key_rows = cur_ref.shape[0] // group
    row = lax.broadcasted_iota(jnp.int32, (tokens, HD), 0)

    def mix(query, kv):
        scores = (
            lax.dot_general(query, kv[:, :HD], nt, preferred_element_type=jnp.float32) * SCALE
        )
        e = jnp.exp(scores - jnp.max(scores, axis=1, keepdims=True))
        weights = (e * (1.0 / jnp.sum(e, axis=1, keepdims=True))).astype(jnp.bfloat16)
        return lax.dot_general(weights, kv[:, HD:], nn, preferred_element_type=jnp.float32)

    for b in range(group):
        here = pl.ds(b * tokens, tokens)
        if b:
            previous = cur_ref[pl.ds((b - 1) * key_rows, key_rows), :]
        else:
            previous = jnp.where(step == 0, carried_ref[...], prev_ref[...])
        query = jnp.concatenate([q_ref[here, pl.ds(h * HD, HD)] for h in range(heads)], axis=0)
        leading = mix(query, previous)
        leading = jnp.where(
            allowed_ref[step * group + b] > 0, leading, jnp.zeros_like(leading)
        )
        tail = pl.ds((b + 1) * tokens - 8, 8)
        final = jnp.concatenate(
            [q_ref[tail, pl.ds(h * HD, HD)].astype(jnp.float32)[7:8] for h in range(heads)], axis=0
        ).astype(jnp.bfloat16)
        trailing = mix(final, cur_ref[pl.ds(b * key_rows, key_rows), :])
        for h in range(heads):
            out_ref[here, pl.ds(h * HD, HD)] = jnp.where(
                row == tokens - 1,
                jnp.broadcast_to(trailing[h : h + 1], (tokens, HD)),
                leading[h * tokens : (h + 1) * tokens],
            ).astype(jnp.bfloat16)


def attend(allowed, queries, keys_values, carried, key_rows):
    block_count = allowed.shape[0]
    group = GROUP
    tokens = queries.shape[0] // block_count
    heads = queries.shape[1] // HD
    return pl.pallas_call(
        functools.partial(attend_body, heads, group),
        out_shape=jax.ShapeDtypeStruct(queries.shape, jnp.bfloat16),
        grid=(block_count // group,),
        in_specs=[
            pl.BlockSpec(memory_space=pltpu.SMEM),
            pl.BlockSpec((group * tokens, queries.shape[1]), lambda c: (c, 0)),
            pl.BlockSpec((group * key_rows, 2 * HD), lambda c: (c, 0)),
            pl.BlockSpec((key_rows, 2 * HD), lambda c: (jnp.maximum(group * c - 1, 0), 0)),
            pl.BlockSpec((key_rows, 2 * HD), lambda c: (0, 0)),
        ],
        out_specs=pl.BlockSpec((group * tokens, queries.shape[1]), lambda c: (c, 0)),
        compiler_params=pltpu.CompilerParams(dimension_semantics=("arbitrary",)),
        name="attend",
    )(allowed, queries, keys_values, keys_values, carried)


def parts(
    db_tokens,
    db_parent,
    db_depth,
    nb_rows,
    seq_start,
    table,
    depth_table,
    enc_gain,
    enc_qkv,
    tree_bias,
    enc_wo,
    cond_kv,
    queries,
    cca_kv,
):
    seq_size = math.prod(lax.axis_size(axis) for axis in SEQ)
    tp_size = lax.axis_size("tp")
    here = lax.axis_index("tp")
    block_count, pair_count = nb_rows.shape
    unit_count = block_count * pair_count
    stored, length = db_tokens.shape
    columns = table.shape[1]
    rows_here = enc_qkv.shape[0]
    kv_cols = cca_kv.shape[2]
    cond_len = cond_kv.shape[0] // block_count
    my_units = unit_count // tp_size
    my_tokens = cond_kv.shape[0] // tp_size
    key_rows = pair_count * length

    flat_rows = nb_rows.reshape(unit_count)
    holder = flat_rows // stored
    local_row = flat_rows % stored
    places = jnp.arange(seq_size, dtype=jnp.int32)
    request = jnp.sum(
        jnp.where(holder[None, :] == places[:, None], local_row[None, :], 0), axis=1
    )
    request = jnp.broadcast_to(request[:, None], (seq_size, 16))

    share = jnp.concatenate(
        [
            enc_qkv.transpose(1, 0, 2).reshape(3 * rows_here, columns),
            enc_wo.T,
            cca_kv.reshape(rows_here, columns),
        ],
        axis=0,
    )[None]
    share = doubled(share, "z", 4)
    share = doubled(share, "z", 2)
    wanted = exchange(request, SEQ)[:, 0]
    share = doubled(share, "z", 1)
    reply = jnp.concatenate(
        [
            jnp.take(db_tokens, wanted, axis=0),
            jnp.take(db_depth, wanted, axis=0),
            jnp.take(db_parent, wanted, axis=0),
        ],
        axis=1,
    )
    fetched = exchange(reply, SEQ)
    z_count = lax.axis_size("z")
    shares = lax.all_gather(
        share.reshape(z_count * 5 * rows_here, columns), ("tp", "y", "core"), axis=0
    ).reshape(tp_size, seq_size, 5 * rows_here, columns)
    cond = exchange(cond_kv.reshape(tp_size, my_tokens, 2 * columns), "tp")

    fetched = jnp.take(fetched, holder, axis=0)
    tokens = fetched[:, :length].reshape(unit_count * length)
    depths = fetched[:, length : 2 * length].reshape(unit_count * length)
    parents = fetched[:, 2 * length :]
    depth_hit = (
        depths[:, None] == jnp.arange(depth_table.shape[0], dtype=jnp.int32)[None, :]
    ).astype(jnp.bfloat16)
    embedded = (
        jnp.take(table, tokens, axis=0).astype(jnp.float32)
        + jnp.dot(depth_hit, depth_table, preferred_element_type=jnp.float32)
    ).astype(jnp.bfloat16)
    pieces = exchange(embedded.reshape(tp_size, my_units * length, columns), "tp")
    slot = jnp.arange(seq_size, dtype=jnp.int32)
    flip = slot % z_count
    flip = 4 * (flip & 1) + (flip & 2) + flip // 4
    place = ((lax.axis_index("z") ^ flip) * (seq_size // z_count) + slot // z_count)[None]
    parents = lax.dynamic_slice_in_dim(parents, here * my_units, my_units)
    parent_hit = (
        parents.reshape(my_units * length)[:, None] == jnp.arange(length, dtype=parents.dtype)[None, :]
    ).astype(jnp.bfloat16)
    outgoing = encoder(
        place,
        jnp.arange(tp_size, dtype=jnp.int32),
        tree_bias,
        pieces,
        enc_gain[None],
        parent_hit,
        cond,
        [("a", shares, 3 * SHARE, 0), ("o", shares, SHARE, 3), ("c", shares, SHARE, 4)],
        my_units,
        length,
        cond_len,
    )
    keys_values = exchange(outgoing, "tp").reshape(unit_count * length, 2 * kv_cols)
    carried = lax.ppermute(
        keys_values[(block_count - 1) * key_rows :], SEQ, [(s, s + 1) for s in range(seq_size - 1)]
    )
    block_index = lax.axis_index(SEQ) * block_count + jnp.arange(block_count, dtype=jnp.int32)
    allowed = (block_index > 0) & (seq_start == 0)
    return attend(allowed.astype(jnp.int32), queries, keys_values, carried, key_rows)


def solution(mesh):
    split = Mesh(
        mesh.devices.reshape(8, 4, 2, mesh.shape["tp"]),
        SEQ + ("tp",),
    )
    in_specs = (
        P(SEQ, None),
        P(SEQ, None),
        P(SEQ, None),
        P(SEQ, None),
        P(SEQ),
        P(None, "tp"),
        P(None, "tp"),
        P(),
        P(SEQ, None, "tp"),
        P(),
        P("tp", SEQ),
        P(SEQ, None, "tp"),
        P(SEQ, "tp"),
        P(SEQ, None, "tp"),
    )
    out_specs = P(SEQ, "tp")
    return jax.shard_map(parts, mesh=split, in_specs=in_specs, out_specs=out_specs, check_vma=False)
```

profile of v0, /device:TPU:32, one launch (start us, length us, event | category | flops | bytes accessed | tf_op | source)
XLA Modules:
  0.0 165.4 jit_solution(5897327483047370128)
XLA Ops:
  6.5 0.0 copy-start
  6.5 0.0 copy-start.5
  6.5 0.0 all-gather.2.cloned.1.call-start
  6.5 0.7 copy.33
  7.3 0.8 maximum_bitcast_fusion
  8.0 6.3 %collective-permute-start = (bf16[1,80,256]{2,1,0:T(8,128)(2,1)S(1)}, bf16[1,80,256]{2,1,0:T(8,128)(2,1)S(1)}, u32[]{:S(2)}, u32[]{:S(2)}) collective-permute-start(bf16[1,80,256]{2,1,0:T(8,128)(2,1)S(1)} %maximum_bitcast_fusion), channel_id=1, source_target_pairs={{0,128},{32,160},{64,192},{96,224},{128,0},{160,32},{192,64},{224,... | collective-permute-start | bytes 122888 | tf_op jit(solution)/shard_map/ppermute | solution.py:26
  14.3 2.0 %collective-permute-done = bf16[1,80,256]{2,1,0:T(8,128)(2,1)S(1)} collective-permute-done((bf16[1,80,256]{2,1,0:T(8,128)(2,1)S(1)}, bf16[1,80,256]{2,1,0:T(8,128)(2,1)S(1)}, u32[]{:S(2)}, u32[]{:S(2)}) %collective-permute-start) | collective-permute-done | bytes 40992 | tf_op jit(solution)/shard_map/ppermute | solution.py:26
  16.3 3.0 %collective-permute-start.1 = (bf16[2,80,256]{2,1,0:T(8,128)(2,1)S(1)}, bf16[2,80,256]{2,1,0:T(8,128)(2,1)S(1)}, u32[]{:S(2)}, u32[]{:S(2)}) collective-permute-start(bf16[2,80,256]{2,1,0:T(8,128)(2,1)S(1)} %pad_maximum_fusion.2), channel_id=1, source_target_pairs={{0,64},{32,96},{64,0},{96,32},{128,192},{160,224},{192,128},{224,1... | collective-permute-start | bytes 245768 | tf_op jit(solution)/shard_map/ppermute | solution.py:26
  19.3 2.5 %collective-permute-done.1 = bf16[2,80,256]{2,1,0:T(8,128)(2,1)S(1)} collective-permute-done((bf16[2,80,256]{2,1,0:T(8,128)(2,1)S(1)}, bf16[2,80,256]{2,1,0:T(8,128)(2,1)S(1)}, u32[]{:S(2)}, u32[]{:S(2)}) %collective-permute-start.1) | collective-permute-done | bytes 81952 | tf_op jit(solution)/shard_map/ppermute | solution.py:26
  21.9 2.3 %collective-permute-start.2 = (bf16[4,80,256]{2,1,0:T(8,128)(2,1)S(1)}, bf16[4,80,256]{2,1,0:T(8,128)(2,1)S(1)}, u32[]{:S(2)}, u32[]{:S(2)}) collective-permute-start(bf16[4,80,256]{2,1,0:T(8,128)(2,1)S(1)} %pad_maximum_fusion.1), channel_id=1, source_target_pairs={{0,32},{32,0},{64,96},{96,64},{128,160},{160,128},{192,224},{224,1... | collective-permute-start | bytes 491528 | tf_op jit(solution)/shard_map/ppermute | solution.py:26
  24.2 3.3 %collective-permute-done.2 = bf16[4,80,256]{2,1,0:T(8,128)(2,1)S(1)} collective-permute-done((bf16[4,80,256]{2,1,0:T(8,128)(2,1)S(1)}, bf16[4,80,256]{2,1,0:T(8,128)(2,1)S(1)}, u32[]{:S(2)}, u32[]{:S(2)}) %collective-permute-start.2) | collective-permute-done | bytes 163872 | tf_op jit(solution)/shard_map/ppermute | solution.py:26
  27.5 0.8 pad_maximum_fusion
  28.3 0.0 all-gather.2.cloned.1.call-update
  28.3 0.8 copy.25
  29.0 0.1 reshape.329
  29.1 0.1 select_reduce_fusion
  29.2 0.8 broadcast_in_dim.62
  30.0 12.0 %all-to-all-start = ((s32[64,1,16]{2,1,0:T(1,128)}), s32[64,1,16]{2,1,0:T(1,128)S(1)}, u32[]{:S(2)}, u32[]{:S(2)}) async-start(s32[64,1,16]{2,1,0:T(1,128)} %broadcast_in_dim.62), calls=%async_computation | async-start | bytes 65536 | tf_op jit(solution)/shard_map/all_to_all | solution.py:21
  42.0 0.1 reshape.330
  42.0 8.5 %all-to-all-done = s32[64,1,16]{2,1,0:T(1,128)S(1)} async-done(((s32[64,1,16]{2,1,0:T(1,128)}), s32[64,1,16]{2,1,0:T(1,128)S(1)}, u32[]{:S(2)}, u32[]{:S(2)}) %all-to-all-start) | async-done | bytes 4128 | tf_op jit(solution)/shard_map/all_to_all | solution.py:21
  50.5 0.1 slice_reduce_fusion
  50.7 0.0 copy-done
  50.7 0.6 gather_fusion.2
  51.3 1.5 gather_fusion.3
  52.8 1.5 gather_fusion.4
  54.4 0.1 broadcast_select_fusion.2
  54.5 0.7 copy.26
  55.2 5.5 %all-to-all-start.1 = ((s32[64,1,384]{2,1,0:T(1,128)}), s32[64,1,384]{2,1,0:T(1,128)S(1)}, u32[]{:S(2)}, u32[]{:S(2)}) async-start(s32[64,1,384]{2,1,0:T(1,128)} %copy.26), calls=%async_computation.1 | async-start | bytes 196608 | tf_op jit(solution)/shard_map/all_to_all | solution.py:21
  60.8 0.0 copy-start.1
  60.8 0.0 copy-start.2
  60.8 2.2 %reshape.334 = bf16[4,128,512]{2,1,0:T(8,128)(2,1)} reshape(bf16[512,2,256]{2,1,0:T(2,128)(2,1)} %param.27) | data formatting | bytes 1048576 | tf_op jit(solution)/shard_map/reshape | solution.py:303
  63.0 7.4 %all-to-all-done.1 = s32[64,1,384]{2,1,0:T(1,128)S(1)} async-done(((s32[64,1,384]{2,1,0:T(1,128)}), s32[64,1,384]{2,1,0:T(1,128)S(1)}, u32[]{:S(2)}, u32[]{:S(2)}) %all-to-all-start.1) | async-done | bytes 98336 | tf_op jit(solution)/shard_map/all_to_all | solution.py:21
  70.4 4.3 %all-to-all-start.3 = ((bf16[4,128,512]{2,1,0:T(8,128)(2,1)}), bf16[4,128,512]{2,1,0:T(8,128)(2,1)S(1)}, u32[]{:S(2)}, u32[]{:S(2)}) async-start(bf16[4,128,512]{2,1,0:T(8,128)(2,1)} %reshape.334), calls=%async_computation.3 | async-start | bytes 1048576 | tf_op jit(solution)/shard_map/all_to_all | solution.py:21
  74.7 0.6 gather_fusion
  75.3 0.1 broadcast_select_fusion.3
  75.4 11.4 %gather_fusion.1 = bf16[2048,256]{1,0:T(8,128)(2,1)S(1)} fusion(bf16[16384,256]{1,0:T(8,128)(2,1)} %param.21, s32[2048]{0:T(1024)S(1)} %broadcast_clamp_fusion), kind=kCustom, calls=%fused_computation.4 | custom fusion | bytes 2105344 | tf_op jit(solution)/shard_map/jit(_take)/gather | solution.py:313
  86.8 0.0 copy-done.5
  86.8 2.8 %fusion = bf16[2048,256]{1,0:T(8,128)(2,1)} fusion(bf16[32,256]{1,0:T(8,128)(2,1)S(1)} %copy-done.5, bf16[2048,256]{1,0:T(8,128)(2,1)S(1)} %gather_fusion.1, pred[2048]{0:T(1024)(128)(4,1)S(1)} %compare_and_fusion, s32[2048]{0:T(1024)S(1)} %get-tuple-element.9), kind=kOutput, calls=%fused_computation.6 | convolution fusion | flops 35717120 | bytes 2123776 | tf_op jit(solution)/shard_map/dot_general | solution.py:314
  89.6 1.2 all-to-all-done.3.cond_ref
  90.9 3.5 %all-to-all-start.2 = ((bf16[4,512,256]{2,1,0:T(8,128)(2,1)}), bf16[4,512,256]{2,1,0:T(8,128)(2,1)S(1)}, u32[]{:S(2)}, u32[]{:S(2)}) async-start(bf16[4,512,256]{2,1,0:T(8,128)(2,1)} %bitcast.7), calls=%async_computation.2 | async-start | bytes 2097152 | tf_op jit(solution)/shard_map/all_to_all | solution.py:21
  94.4 0.1 fusion.2.hit_ref
  94.6 14.7 %all-to-all-done.2.emb_ref = bf16[4,512,256]{2,1,0:T(8,128)(2,1)S(1)} async-done(((bf16[4,512,256]{2,1,0:T(8,128)(2,1)}), bf16[4,512,256]{2,1,0:T(8,128)(2,1)S(1)}, u32[]{:S(2)}, u32[]{:S(2)}) %all-to-all-start.2) | async-done | bytes 1048608 | tf_op jit(solution)/shard_map/all_to_all | solution.py:21
  109.3 0.0 all-gather.2.cloned.1.call-done
  109.3 0.0 copy-done.1
  109.3 0.0 copy-done.2
  109.3 0.0 copy-start.6
  109.3 17.2 %encoder.1 = bf16[4,512,256]{2,1,0:T(8,128)(2,1)} custom-call(s32[1,64]{1,0:T(1,128)S(1)} %fusion.3.place_ref, s32[4]{0:T(128)S(1)} %iota.27.xs_ref, f32[8]{0:T(128)S(1)} %copy-done.2, bf16[4,512,256]{2,1,0:T(8,128)(2,1)S(1)} %all-to-all-done.2.emb_ref, f32[1,1024]{1,0:T(1,128)S(1)} %bitcast.34, bf16[512,128]{1,0:T(8,128)(2,1)S(1)} %fusion.2.hit_ref, ...), custom_call_target="tpu_custom_call" | custom-call | tf_op jit(solution)/shard_map/encoder/pallas_call | solution.py:141
  126.5 3.5 %all-to-all-start.4 = ((bf16[4,512,256]{2,1,0:T(8,128)(2,1)}), bf16[4,512,256]{2,1,0:T(8,128)(2,1)S(1)}, u32[]{:S(2)}, u32[]{:S(2)}) async-start(bf16[4,512,256]{2,1,0:T(8,128)(2,1)} %encoder.1), calls=%async_computation.4 | async-start | bytes 2097152 | tf_op jit(solution)/shard_map/all_to_all | solution.py:21
  130.0 14.0 %all-to-all-done.4 = bf16[4,512,256]{2,1,0:T(8,128)(2,1)S(1)} async-done(((bf16[4,512,256]{2,1,0:T(8,128)(2,1)}), bf16[4,512,256]{2,1,0:T(8,128)(2,1)S(1)}, u32[]{:S(2)}, u32[]{:S(2)}) %all-to-all-start.4) | async-done | bytes 1048608 | tf_op jit(solution)/shard_map/all_to_all | solution.py:21
  144.0 0.0 copy-start.3
  144.0 1.9 %collective-permute-start.3 = (bf16[256,256]{1,0:T(8,128)(2,1)S(1)}, bf16[256,256]{1,0:T(8,128)(2,1)S(1)}, u32[]{:S(2)}, u32[]{:S(2)}) collective-permute-start(bf16[256,256]{1,0:T(8,128)(2,1)S(1)} %slice.34), channel_id=1, source_target_pairs={{0,4},{4,8},{8,12},{12,16},{16,20},{20,24},{24,28},{28,32},{32,36}... | collective-permute-start | bytes 393224 | tf_op jit(solution)/shard_map/ppermute | solution.py:339
  145.9 0.0 copy-done.6
  145.9 0.5 and_convert_fusion.allowed_ref
  146.5 5.9 %collective-permute-done.3.carried_ref = bf16[256,256]{1,0:T(8,128)(2,1)S(1)} collective-permute-done((bf16[256,256]{1,0:T(8,128)(2,1)S(1)}, bf16[256,256]{1,0:T(8,128)(2,1)S(1)}, u32[]{:S(2)}, u32[]{:S(2)}) %collective-permute-start.3) | collective-permute-done | bytes 131104 | tf_op jit(solution)/shard_map/ppermute | solution.py:339
  152.4 0.0 copy-done.3
  152.4 0.0 copy-start.4
  152.4 0.6 copy-done.4
  153.0 5.5 %attend.1 = bf16[512,1024]{1,0:T(8,128)(2,1)} custom-call(s32[8]{0:T(128)} %and_convert_fusion.allowed_ref, bf16[512,1024]{1,0:T(8,128)(2,1)} %q_ref.1, bf16[2048,256]{1,0:T(8,128)(2,1)} %bitcast.39, bf16[2048,256]{1,0:T(8,128)(2,1)} %bitcast.40, bf16[256,256]{1,0:T(8,128)(2,1)} %copy-done.4), custom_call_target="tpu_custom_call" | custom-call | tf_op jit(solution)/shard_map/attend/pallas_call | solution.py:222
  (19 shorter events, 0.2 us)
Async XLA Ops:
  6.5 44.1 %copy-start = (s32[512,128]{1,0:T(8,128)S(1)}, s32[512,128]{1,0:T(8,128)}, u32[]{:S(2)}) copy-start(s32[512,128]{1,0:T(8,128)} %param.16) | copy-start | bytes 786436
  6.5 80.3 %copy-start.5 = (bf16[32,256]{1,0:T(8,128)(2,1)S(1)}, bf16[32,256]{1,0:T(8,128)(2,1)}, u32[]{:S(2)}) copy-start(bf16[32,256]{1,0:T(8,128)(2,1)} %param.22) | copy-start | bytes 49156
  6.5 102.7 %all-gather.2.cloned.1.call-start = ((), (), s32[]{:S(2)}) async-start(), calls=%async_computation.5 | async-start | bytes 10813440 | tf_op jit(solution)/shard_map/all_gather | solution.py:300
  8.0 8.3 %collective-permute-start = (bf16[1,80,256]{2,1,0:T(8,128)(2,1)S(1)}, bf16[1,80,256]{2,1,0:T(8,128)(2,1)S(1)}, u32[]{:S(2)}, u32[]{:S(2)}) collective-permute-start(bf16[1,80,256]{2,1,0:T(8,128)(2,1)S(1)} %maximum_bitcast_fusion), channel_id=1, source_target_pairs={{0,128},{32,160},{64,192},{96,224},{128,0},{160,32},{192,64},{224,... | collective-permute-start | bytes 122888 | tf_op jit(solution)/shard_map/ppermute | solution.py:26
  16.3 5.5 %collective-permute-start.1 = (bf16[2,80,256]{2,1,0:T(8,128)(2,1)S(1)}, bf16[2,80,256]{2,1,0:T(8,128)(2,1)S(1)}, u32[]{:S(2)}, u32[]{:S(2)}) collective-permute-start(bf16[2,80,256]{2,1,0:T(8,128)(2,1)S(1)} %pad_maximum_fusion.2), channel_id=1, source_target_pairs={{0,64},{32,96},{64,0},{96,32},{128,192},{160,224},{192,128},{224,1... | collective-permute-start | bytes 245768 | tf_op jit(solution)/shard_map/ppermute | solution.py:26
  21.9 5.6 %collective-permute-start.2 = (bf16[4,80,256]{2,1,0:T(8,128)(2,1)S(1)}, bf16[4,80,256]{2,1,0:T(8,128)(2,1)S(1)}, u32[]{:S(2)}, u32[]{:S(2)}) collective-permute-start(bf16[4,80,256]{2,1,0:T(8,128)(2,1)S(1)} %pad_maximum_fusion.1), channel_id=1, source_target_pairs={{0,32},{32,0},{64,96},{96,64},{128,160},{160,128},{192,224},{224,1... | collective-permute-start | bytes 491528 | tf_op jit(solution)/shard_map/ppermute | solution.py:26
  30.0 20.5 %all-to-all-start = ((s32[64,1,16]{2,1,0:T(1,128)}), s32[64,1,16]{2,1,0:T(1,128)S(1)}, u32[]{:S(2)}, u32[]{:S(2)}) async-start(s32[64,1,16]{2,1,0:T(1,128)} %broadcast_in_dim.62), calls=%async_computation | async-start | bytes 65536 | tf_op jit(solution)/shard_map/all_to_all | solution.py:21
  55.2 15.2 %all-to-all-start.1 = ((s32[64,1,384]{2,1,0:T(1,128)}), s32[64,1,384]{2,1,0:T(1,128)S(1)}, u32[]{:S(2)}, u32[]{:S(2)}) async-start(s32[64,1,384]{2,1,0:T(1,128)} %copy.26), calls=%async_computation.1 | async-start | bytes 196608 | tf_op jit(solution)/shard_map/all_to_all | solution.py:21
  60.8 48.5 %copy-start.1 = (f32[1024]{0:T(1024)S(1)}, f32[1024]{0:T(1024)}, u32[]{:S(2)}) copy-start(f32[1024]{0:T(1024)} %param.23) | copy-start | bytes 12292
  60.8 48.5 %copy-start.2 = (f32[8]{0:T(128)S(1)}, f32[8]{0:T(128)}, u32[]{:S(2)}) copy-start(f32[8]{0:T(128)} %bias_ref.1) | copy-start | bytes 100
  70.4 20.5 %all-to-all-start.3 = ((bf16[4,128,512]{2,1,0:T(8,128)(2,1)}), bf16[4,128,512]{2,1,0:T(8,128)(2,1)S(1)}, u32[]{:S(2)}, u32[]{:S(2)}) async-start(bf16[4,128,512]{2,1,0:T(8,128)(2,1)} %reshape.334), calls=%async_computation.3 | async-start | bytes 1048576 | tf_op jit(solution)/shard_map/all_to_all | solution.py:21
  90.9 18.4 %all-to-all-start.2 = ((bf16[4,512,256]{2,1,0:T(8,128)(2,1)}), bf16[4,512,256]{2,1,0:T(8,128)(2,1)S(1)}, u32[]{:S(2)}, u32[]{:S(2)}) async-start(bf16[4,512,256]{2,1,0:T(8,128)(2,1)} %bitcast.7), calls=%async_computation.2 | async-start | bytes 2097152 | tf_op jit(solution)/shard_map/all_to_all | solution.py:21
  109.3 36.6 %copy-start.6 = (s32[8]{0:T(128)S(1)}, s32[8]{0:T(128)}, u32[]{:S(2)}) copy-start(s32[8]{0:T(128)} %param.20) | copy-start | bytes 100
  126.5 17.5 %all-to-all-start.4 = ((bf16[4,512,256]{2,1,0:T(8,128)(2,1)}), bf16[4,512,256]{2,1,0:T(8,128)(2,1)S(1)}, u32[]{:S(2)}, u32[]{:S(2)}) async-start(bf16[4,512,256]{2,1,0:T(8,128)(2,1)} %encoder.1), calls=%async_computation.4 | async-start | bytes 2097152 | tf_op jit(solution)/shard_map/all_to_all | solution.py:21
  144.0 8.4 %copy-start.3 = (bf16[4,512,256]{2,1,0:T(8,128)(2,1)}, bf16[4,512,256]{2,1,0:T(8,128)(2,1)S(1)}, u32[]{:S(2)}) copy-start(bf16[4,512,256]{2,1,0:T(8,128)(2,1)S(1)} %all-to-all-done.4) | copy-start | bytes 3145732
  144.0 8.4 %collective-permute-start.3 = (bf16[256,256]{1,0:T(8,128)(2,1)S(1)}, bf16[256,256]{1,0:T(8,128)(2,1)S(1)}, u32[]{:S(2)}, u32[]{:S(2)}) collective-permute-start(bf16[256,256]{1,0:T(8,128)(2,1)S(1)} %slice.34), channel_id=1, source_target_pairs={{0,4},{4,8},{8,12},{12,16},{16,20},{20,24},{24,28},{28,32},{32,36}... | collective-permute-start | bytes 393224 | tf_op jit(solution)/shard_map/ppermute | solution.py:339
  152.4 0.7 copy-start.4
Sparse Core Ops, SparseCore 0:
  28.4 70.8 all-gather.1
where the time goes:
time: 167 us; the launch traced here: 165 us
  waiting for transfers between devices  59.6 us (36%)
  starting transfers between devices  42.3 us (25%)
  Pallas kernels  22.7 us (14%)
  local copies, waits for them, and re-layouts  21.8 us (13%)
  between operations  13.6 us (8%)
  matrix products  2.8 us (2%)
  other arithmetic  2.54 us (2%)
    all_to_all x5, waiting for transfers between devices, exchange(): return lax.all_to_all(value, axis, split_axis=0, concat_axis=0, tiled=True)  45.8 us
    all_to_all x5, starting transfers between devices, exchange(): return lax.all_to_all(value, axis, split_axis=0, concat_axis=0, tiled=True)  28.8 us
    pallas_call x1, Pallas kernels, encoder(): pl.pallas_call(functools.partial(encoder_body, parts, my_units, length, c...  17.2 us
    ppermute x3, starting transfers between devices, swapped(): return lax.ppermute(value, axis, [(i, i ^ distance) for i in range(count)])  11.6 us
    gather x1, local copies, waits for them, and re-layouts, parts(): jnp.take(table, tokens, axis=0).astype(jnp.float32)  11.4 us
    ppermute x3, waiting for transfers between devices, swapped(): return lax.ppermute(value, axis, [(i, i ^ distance) for i in range(count)])  7.82 us
    ppermute x1, waiting for transfers between devices, parts(): lax.ppermute(keys_values[(block_count - 1) * key_rows:], SEQ, [(s, s + 1)...  5.94 us
    pallas_call x1, Pallas kernels, attend(): pl.pallas_call(functools.partial(attend_body, heads, group), out_shape=ja...  5.54 us
  transfers between devices with their start and end apart: 10, of which 9 were waited for; matrix products, arithmetic and copies ran while one was open for 15% of the time, Pallas kernels for 0%

commit v1 on v0

--- a/solution.py
+++ b/solution.py
@@ -15,10 +15,16 @@
 
 
 SEQ = ("z", "y", "core")
+TURNS = (0, 1, -1, 2)
 
 
 def exchange(value, axis):
     return lax.all_to_all(value, axis, split_axis=0, concat_axis=0, tiled=True)
+
+
+def moved(value, axis, steps):
+    count = lax.axis_size(axis)
+    return lax.ppermute(value, axis, [(i, (i + steps) % count) for i in range(count)])
 
 
 def swapped(value, axis, distance):
@@ -67,7 +73,7 @@
 
     @pl.when(step < pieces)
     def _():
-        head = xs_ref[step] * (columns // HD)
+        head = step * (columns // HD)
         assemble(wa_refs, place_ref, buf_ref, 0, 3)
         assemble(wo_refs, place_ref, buf_ref, 3, 1)
         normed = normed_ref[...]
@@ -150,14 +156,14 @@
                 full(gain.shape),
                 full(hit.shape),
                 pl.BlockSpec(
-                    (1,) + cond.shape[1:], lambda i, p, x: (jnp.minimum(i, last), 0, 0)
+                    (1,) + cond.shape[1:], lambda i, p, x: (x[jnp.minimum(i, last)], 0, 0)
                 ),
                 *specs["a"],
                 *specs["o"],
                 *specs["c"],
             ],
             out_specs=pl.BlockSpec(
-                (1, rows, columns), lambda i, p, x: (x[jnp.maximum(i - pieces, 0)], 0, 0)
+                (1, rows, columns), lambda i, p, x: (jnp.maximum(i - pieces, 0), 0, 0)
             ),
             scratch_shapes=[
                 pltpu.VMEM((rows, width), jnp.bfloat16),
@@ -284,9 +290,8 @@
         axis=0,
     )[None]
     share = doubled(share, "z", 4)
-    share = doubled(share, "z", 2)
+    share = jnp.concatenate([share] + [moved(share, "z", d) for d in TURNS[1:]], axis=0)
     wanted = exchange(request, SEQ)[:, 0]
-    share = doubled(share, "z", 1)
     reply = jnp.concatenate(
         [
             jnp.take(db_tokens, wanted, axis=0),
@@ -295,13 +300,25 @@
         ],
         axis=1,
     )
+    reply, pieces_here = lax.optimization_barrier(
+        (reply, cond_kv.reshape(tp_size, my_tokens, 2 * columns))
+    )
     fetched = exchange(reply, SEQ)
     z_count = lax.axis_size("z")
     shares = lax.all_gather(
         share.reshape(z_count * 5 * rows_here, columns), ("tp", "y", "core"), axis=0
     ).reshape(tp_size, seq_size, 5 * rows_here, columns)
-    cond = exchange(cond_kv.reshape(tp_size, my_tokens, 2 * columns), "tp")
-
+    cond = jnp.stack(
+        [lax.dynamic_index_in_dim(pieces_here, here, 0, keepdims=False)]
+        + [
+            moved(
+                lax.dynamic_index_in_dim(pieces_here, (here + d) % tp_size, 0, keepdims=False),
+                "tp",
+                d,
+            )
+            for d in range(1, tp_size)
+        ]
+    )
     fetched = jnp.take(fetched, holder, axis=0)
     tokens = fetched[:, :length].reshape(unit_count * length)
     depths = fetched[:, length : 2 * length].reshape(unit_count * length)
@@ -315,16 +332,16 @@
     ).astype(jnp.bfloat16)
     pieces = exchange(embedded.reshape(tp_size, my_units * length, columns), "tp")
     slot = jnp.arange(seq_size, dtype=jnp.int32)
-    flip = slot % z_count
-    flip = 4 * (flip & 1) + (flip & 2) + flip // 4
-    place = ((lax.axis_index("z") ^ flip) * (seq_size // z_count) + slot // z_count)[None]
+    turn = jnp.array(TURNS, jnp.int32)[slot % z_count // 2]
+    z_of = (lax.axis_index("z") + (z_count // 2) * (slot % 2) - turn) % z_count
+    place = (z_of * (seq_size // z_count) + slot // z_count)[None]
     parents = lax.dynamic_slice_in_dim(parents, here * my_units, my_units)
     parent_hit = (
         parents.reshape(my_units * length)[:, None] == jnp.arange(length, dtype=parents.dtype)[None, :]
     ).astype(jnp.bfloat16)
     outgoing = encoder(
         place,
-        jnp.arange(tp_size, dtype=jnp.int32),
+        (here - jnp.arange(tp_size, dtype=jnp.int32)) % tp_size,
         tree_bias,
         pieces,
         enc_gain[None],

time: 167 us -> 166 us (level)
  starting transfers between devices: 42.3 us -> 44.1 us
  waiting for transfers between devices: 59.6 us -> 57.9 us
    ppermute x0 -> x6, waiting for transfers between devices: none -> 19.5 us  [moved(): lax.ppermute(value, axis, [(i, (i + steps) % count) for i in range(count)])]
    all_to_all x5 -> x4, waiting for transfers between devices: 45.8 us -> 31.2 us  [exchange(): return lax.all_to_all(value, axis, split_axis=0, concat_axis=0, tiled=True)]
    ppermute x0 -> x6, starting transfers between devices: none -> 11.1 us  [moved(): lax.ppermute(value, axis, [(i, (i + steps) % count) for i in range(count)])]
    ppermute x3 -> x1, waiting for transfers between devices: 7.82 us -> 1.23 us  [swapped(): return lax.ppermute(value, axis, [(i, i ^ distance) for i in range(count)])]
    ppermute x3 -> x1, starting transfers between devices: 11.6 us -> 6.29 us  [swapped(): return lax.ppermute(value, axis, [(i, i ^ distance) for i in range(count)])]
    all_to_all x5 -> x4, starting transfers between devices: 28.8 us -> 24.7 us  [exchange(): return lax.all_to_all(value, axis, split_axis=0, concat_axis=0, tiled=True)]
  transfers between devices with their start and end apart: 10 -> 13, of which waited for: 9 -> 9; matrix products, arithmetic and copies ran while one was open for 15% -> 15% of each run, Pallas kernels for 0% -> 0%
where the time goes in v1:
time: 166 us; the launch traced here: 165 us
  waiting for transfers between devices  57.9 us (35%)
  starting transfers between devices  44.1 us (27%)
  Pallas kernels  22.6 us (14%)
  local copies, waits for them, and re-layouts  21.6 us (13%)
  between operations  13.7 us (8%)
  matrix products  2.8 us (2%)
  other arithmetic  2.63 us (2%)
    all_to_all x4, waiting for transfers between devices, exchange(): return lax.all_to_all(value, axis, split_axis=0, concat_axis=0, tiled=True)  31.2 us
    all_to_all x4, starting transfers between devices, exchange(): return lax.all_to_all(value, axis, split_axis=0, concat_axis=0, tiled=True)  24.7 us
    ppermute x6, waiting for transfers between devices, moved(): lax.ppermute(value, axis, [(i, (i + steps) % count) for i in range(count)])  19.5 us
    pallas_call x1, Pallas kernels, encoder(): pl.pallas_call(functools.partial(encoder_body, parts, my_units, length, c...  17.1 us
    gather x1, local copies, waits for them, and re-layouts, parts(): jnp.take(table, tokens, axis=0).astype(jnp.float32)  11.2 us
    ppermute x6, starting transfers between devices, moved(): lax.ppermute(value, axis, [(i, (i + steps) % count) for i in range(count)])  11.1 us
    ppermute x1, starting transfers between devices, swapped(): return lax.ppermute(value, axis, [(i, i ^ distance) for i in range(count)])  6.29 us
    ppermute x1, waiting for transfers between devices, parts(): lax.ppermute(keys_values[(block_count - 1) * key_rows:], SEQ, [(s, s + 1)...  5.92 us
  transfers between devices with their start and end apart: 13, of which 9 were waited for; matrix products, arithmetic and copies ran while one was open for 15% of the time, Pallas kernels for 0%

profile of v1, /device:TPU:32, one launch (start us, length us, event | category | flops | bytes accessed | tf_op | source)
XLA Modules:
  0.0 165.3 jit_solution(12882185905239056852)
XLA Ops:
  6.5 0.0 copy-start
  6.5 0.0 copy-start.6
  6.5 0.0 all-gather.2.cloned.1.call-start
  6.5 0.7 copy.34
  7.3 0.8 maximum_bitcast_fusion
  8.0 6.3 %collective-permute-start.3 = (bf16[1,80,256]{2,1,0:T(8,128)(2,1)S(1)}, bf16[1,80,256]{2,1,0:T(8,128)(2,1)S(1)}, u32[]{:S(2)}, u32[]{:S(2)}) collective-permute-start(bf16[1,80,256]{2,1,0:T(8,128)(2,1)S(1)} %maximum_bitcast_fusion), channel_id=1, source_target_pairs={{0,128},{32,160},{64,192},{96,224},{128,0},{160,32},{192,64},{224,... | collective-permute-start | bytes 122888 | tf_op jit(solution)/shard_map/ppermute | solution.py:32
  14.3 0.8 constant_dynamic-update-slice_fusion.4
  15.1 1.2 collective-permute-done.3
  16.3 1.7 %collective-permute-start.4 = (bf16[2,80,256]{2,1,0:T(8,128)(2,1)S(1)}, bf16[2,80,256]{2,1,0:T(8,128)(2,1)S(1)}, u32[]{:S(2)}, u32[]{:S(2)}) collective-permute-start(bf16[2,80,256]{2,1,0:T(8,128)(2,1)S(1)} %pad_maximum_fusion.1), channel_id=1, source_target_pairs={{0,32},{32,64},{64,96},{96,128},{128,160},{160,192},{192,224},{224... | collective-permute-start | bytes 245768 | tf_op jit(solution)/shard_map/ppermute | solution.py:27
  18.1 0.4 collective-permute-start.5
  18.4 4.0 %collective-permute-start.6 = (bf16[2,80,256]{2,1,0:T(8,128)(2,1)S(1)}, bf16[2,80,256]{2,1,0:T(8,128)(2,1)S(1)}, u32[]{:S(2)}, u32[]{:S(2)}) collective-permute-start(bf16[2,80,256]{2,1,0:T(8,128)(2,1)S(1)} %pad_maximum_fusion.1), channel_id=1, source_target_pairs={{0,64},{32,96},{64,128},{96,160},{128,192},{160,224},{192,0},{224,... | collective-permute-start | bytes 245768 | tf_op jit(solution)/shard_map/ppermute | solution.py:27
  22.5 0.0 collective-permute-done.4
  22.5 0.0 collective-permute-done.5
  22.5 3.7 %collective-permute-done.6 = bf16[2,80,256]{2,1,0:T(8,128)(2,1)S(1)} collective-permute-done((bf16[2,80,256]{2,1,0:T(8,128)(2,1)S(1)}, bf16[2,80,256]{2,1,0:T(8,128)(2,1)S(1)}, u32[]{:S(2)}, u32[]{:S(2)}) %collective-permute-start.6) | collective-permute-done | bytes 81952 | tf_op jit(solution)/shard_map/ppermute | solution.py:27
  26.3 0.7 copy-done.4
  27.0 0.0 all-gather.2.cloned.1.call-update
  27.0 0.8 copy.26
  27.8 0.1 reshape.394
  27.9 0.1 select_reduce_fusion
  28.0 0.8 broadcast_in_dim.63
  28.7 11.3 %all-to-all-start = ((s32[64,1,16]{2,1,0:T(1,128)}), s32[64,1,16]{2,1,0:T(1,128)S(1)}, u32[]{:S(2)}, u32[]{:S(2)}) async-start(s32[64,1,16]{2,1,0:T(1,128)} %broadcast_in_dim.63), calls=%async_computation | async-start | bytes 65536 | tf_op jit(solution)/shard_map/all_to_all | solution.py:22
  40.1 0.1 reshape.396
  40.1 1.4 reshape.395
  41.5 7.1 %all-to-all-done = s32[64,1,16]{2,1,0:T(1,128)S(1)} async-done(((s32[64,1,16]{2,1,0:T(1,128)}), s32[64,1,16]{2,1,0:T(1,128)S(1)}, u32[]{:S(2)}, u32[]{:S(2)}) %all-to-all-start) | async-done | bytes 4128 | tf_op jit(solution)/shard_map/all_to_all | solution.py:22
  48.6 0.1 slice_reduce_fusion
  48.8 0.0 copy-done
  48.8 0.6 gather_fusion.2
  49.4 1.5 gather_fusion.3
  50.9 1.5 gather_fusion.4
  52.5 0.1 broadcast_select_fusion.2
  52.6 0.7 copy.27
  53.3 5.5 %all-to-all-start.1 = ((s32[64,1,384]{2,1,0:T(1,128)}), s32[64,1,384]{2,1,0:T(1,128)S(1)}, u32[]{:S(2)}, u32[]{:S(2)}) async-start(s32[64,1,384]{2,1,0:T(1,128)} %copy.27), calls=%async_computation.1 | async-start | bytes 196608 | tf_op jit(solution)/shard_map/all_to_all | solution.py:22
  58.9 9.6 %all-to-all-done.1 = s32[64,1,384]{2,1,0:T(1,128)S(1)} async-done(((s32[64,1,384]{2,1,0:T(1,128)}), s32[64,1,384]{2,1,0:T(1,128)S(1)}, u32[]{:S(2)}, u32[]{:S(2)}) %all-to-all-start.1) | async-done | bytes 98336 | tf_op jit(solution)/shard_map/all_to_all | solution.py:22
  68.5 0.0 copy-start.1
  68.5 0.0 copy-start.2
  68.6 0.6 gather_fusion
  69.1 0.1 broadcast_select_fusion.3
  69.3 11.2 %gather_fusion.1 = bf16[2048,256]{1,0:T(8,128)(2,1)S(1)} fusion(bf16[16384,256]{1,0:T(8,128)(2,1)} %param.22, s32[2048]{0:T(1024)S(1)} %broadcast_clamp_fusion), kind=kCustom, calls=%fused_computation.4 | custom fusion | bytes 2105344 | tf_op jit(solution)/shard_map/jit(_take)/gather | solution.py:330
  80.5 0.0 copy-done.6
  80.5 2.8 %fusion = bf16[2048,256]{1,0:T(8,128)(2,1)} fusion(bf16[32,256]{1,0:T(8,128)(2,1)S(1)} %copy-done.6, bf16[2048,256]{1,0:T(8,128)(2,1)S(1)} %gather_fusion.1, pred[2048]{0:T(1024)(128)(4,1)S(1)} %compare_and_fusion, s32[2048]{0:T(1024)S(1)} %get-tuple-element.17), kind=kOutput, calls=%fused_computation.6 | convolution fusion | flops 35717120 | bytes 2123776 | tf_op jit(solution)/shard_map/dot_general | solution.py:331
  83.3 4.3 %all-to-all-start.2 = ((bf16[4,512,256]{2,1,0:T(8,128)(2,1)}), bf16[4,512,256]{2,1,0:T(8,128)(2,1)S(1)}, u32[]{:S(2)}, u32[]{:S(2)}) async-start(bf16[4,512,256]{2,1,0:T(8,128)(2,1)} %bitcast.8), calls=%async_computation.2 | async-start | bytes 2097152 | tf_op jit(solution)/shard_map/all_to_all | solution.py:22
  87.7 3.3 %collective-permute-start.2 = (bf16[128,512]{1,0:T(8,128)(2,1)S(1)}, bf16[128,512]{1,0:T(8,128)(2,1)S(1)}, u32[]{:S(2)}, u32[]{:S(2)}) collective-permute-start(bf16[128,512]{1,0:T(8,128)(2,1)S(1)} %get-tuple-element.13), channel_id=1, source_target_pairs={{0,3},{1,0},{2,1},{3,2},{4,7},{5,4},{6,5},{7,6},{8,11},{9,8},{10,9... | collective-permute-start | bytes 393224 | tf_op jit(solution)/shard_map/ppermute | solution.py:27
  91.0 0.9 collective-permute-start.1
  91.8 0.9 collective-permute-start
  92.7 12.7 %collective-permute-done.2 = bf16[128,512]{1,0:T(8,128)(2,1)S(1)} collective-permute-done((bf16[128,512]{1,0:T(8,128)(2,1)S(1)}, bf16[128,512]{1,0:T(8,128)(2,1)S(1)}, u32[]{:S(2)}, u32[]{:S(2)}) %collective-permute-start.2) | collective-permute-done | bytes 131104 | tf_op jit(solution)/shard_map/ppermute | solution.py:27
  105.5 1.5 collective-permute-done.1
  107.0 1.4 collective-permute-done
  108.4 0.1 pad_maximum_fusion.cond_ref
  108.5 0.1 fusion.2.hit_ref
  108.6 0.0 all-to-all-done.2.emb_ref
  108.6 0.0 all-gather.2.cloned.1.call-done
  108.7 0.0 copy-done.1
  108.7 0.0 copy-done.2
  108.7 0.0 copy-start.7
  108.7 17.1 %encoder.1 = bf16[4,512,256]{2,1,0:T(8,128)(2,1)} custom-call(s32[1,64]{1,0:T(1,128)S(1)} %fusion.3.place_ref, s32[4]{0:T(128)S(1)} %and_select_fusion.3.xs_ref, f32[8]{0:T(128)S(1)} %copy-done.2, bf16[4,512,256]{2,1,0:T(8,128)(2,1)S(1)} %all-to-all-done.2.emb_ref, f32[1,1024]{1,0:T(1,128)S(1)} %bitcast.50, bf16[512,128]{1,0:T(8,128)(2,1)S(1)} %fusion.2.hit_ref, ...), custom_call_target="tpu_custom_call" | custom-call | tf_op jit(solution)/shard_map/encoder/pallas_call | solution.py:147
  125.8 3.5 %all-to-all-start.3 = ((bf16[4,512,256]{2,1,0:T(8,128)(2,1)}), bf16[4,512,256]{2,1,0:T(8,128)(2,1)S(1)}, u32[]{:S(2)}, u32[]{:S(2)}) async-start(bf16[4,512,256]{2,1,0:T(8,128)(2,1)} %encoder.1), calls=%async_computation.3 | async-start | bytes 2097152 | tf_op jit(solution)/shard_map/all_to_all | solution.py:22
  129.4 14.6 %all-to-all-done.3 = bf16[4,512,256]{2,1,0:T(8,128)(2,1)S(1)} async-done(((bf16[4,512,256]{2,1,0:T(8,128)(2,1)}), bf16[4,512,256]{2,1,0:T(8,128)(2,1)S(1)}, u32[]{:S(2)}, u32[]{:S(2)}) %all-to-all-start.3) | async-done | bytes 1048608 | tf_op jit(solution)/shard_map/all_to_all | solution.py:22
  143.9 1.9 %collective-permute-start.7 = (bf16[256,256]{1,0:T(8,128)(2,1)S(1)}, bf16[256,256]{1,0:T(8,128)(2,1)S(1)}, u32[]{:S(2)}, u32[]{:S(2)}) collective-permute-start(bf16[256,256]{1,0:T(8,128)(2,1)S(1)} %slice.39), channel_id=1, source_target_pairs={{0,4},{4,8},{8,12},{12,16},{16,20},{20,24},{24,28},{28,32},{32,36}... | collective-permute-start | bytes 393224 | tf_op jit(solution)/shard_map/ppermute | solution.py:356
  145.9 0.0 copy-done.7
  145.9 0.5 and_convert_fusion.allowed_ref
  146.4 5.9 %collective-permute-done.7.carried_ref = bf16[256,256]{1,0:T(8,128)(2,1)S(1)} collective-permute-done((bf16[256,256]{1,0:T(8,128)(2,1)S(1)}, bf16[256,256]{1,0:T(8,128)(2,1)S(1)}, u32[]{:S(2)}, u32[]{:S(2)}) %collective-permute-start.7) | collective-permute-done | bytes 131104 | tf_op jit(solution)/shard_map/ppermute | solution.py:356
  152.3 0.0 copy-done.3
  152.3 0.6 copy-done.5
  153.0 5.5 %attend.1 = bf16[512,1024]{1,0:T(8,128)(2,1)} custom-call(s32[8]{0:T(128)} %and_convert_fusion.allowed_ref, bf16[512,1024]{1,0:T(8,128)(2,1)} %q_ref.1, bf16[2048,256]{1,0:T(8,128)(2,1)} %bitcast.55, bf16[2048,256]{1,0:T(8,128)(2,1)} %bitcast.56, bf16[256,256]{1,0:T(8,128)(2,1)} %copy-done.5), custom_call_target="tpu_custom_call" | custom-call | tf_op jit(solution)/shard_map/attend/pallas_call | solution.py:228
  (26 shorter events, 0.2 us)
Async XLA Ops:
  6.5 42.2 %copy-start = (s32[512,128]{1,0:T(8,128)S(1)}, s32[512,128]{1,0:T(8,128)}, u32[]{:S(2)}) copy-start(s32[512,128]{1,0:T(8,128)} %param.17) | copy-start | bytes 786436
  6.5 73.9 %copy-start.6 = (bf16[32,256]{1,0:T(8,128)(2,1)S(1)}, bf16[32,256]{1,0:T(8,128)(2,1)}, u32[]{:S(2)}) copy-start(bf16[32,256]{1,0:T(8,128)(2,1)} %param.23) | copy-start | bytes 49156
  6.5 102.1 %all-gather.2.cloned.1.call-start = ((), (), s32[]{:S(2)}) async-start(), calls=%async_computation.4 | async-start | bytes 10813440 | tf_op jit(solution)/shard_map/all_gather | solution.py:308
  8.0 8.3 %collective-permute-start.3 = (bf16[1,80,256]{2,1,0:T(8,128)(2,1)S(1)}, bf16[1,80,256]{2,1,0:T(8,128)(2,1)S(1)}, u32[]{:S(2)}, u32[]{:S(2)}) collective-permute-start(bf16[1,80,256]{2,1,0:T(8,128)(2,1)S(1)} %maximum_bitcast_fusion), channel_id=1, source_target_pairs={{0,128},{32,160},{64,192},{96,224},{128,0},{160,32},{192,64},{224,... | collective-permute-start | bytes 122888 | tf_op jit(solution)/shard_map/ppermute | solution.py:32
  16.3 6.1 %collective-permute-start.4 = (bf16[2,80,256]{2,1,0:T(8,128)(2,1)S(1)}, bf16[2,80,256]{2,1,0:T(8,128)(2,1)S(1)}, u32[]{:S(2)}, u32[]{:S(2)}) collective-permute-start(bf16[2,80,256]{2,1,0:T(8,128)(2,1)S(1)} %pad_maximum_fusion.1), channel_id=1, source_target_pairs={{0,32},{32,64},{64,96},{96,128},{128,160},{160,192},{192,224},{224... | collective-permute-start | bytes 245768 | tf_op jit(solution)/shard_map/ppermute | solution.py:27
  18.1 4.4 %collective-permute-start.5 = (bf16[2,80,256]{2,1,0:T(8,128)(2,1)S(1)}, bf16[2,80,256]{2,1,0:T(8,128)(2,1)S(1)}, u32[]{:S(2)}, u32[]{:S(2)}) collective-permute-start(bf16[2,80,256]{2,1,0:T(8,128)(2,1)S(1)} %pad_maximum_fusion.1), channel_id=1, source_target_pairs={{0,224},{32,0},{64,32},{96,64},{128,96},{160,128},{192,160},{224,1... | collective-permute-start | bytes 245768 | tf_op jit(solution)/shard_map/ppermute | solution.py:27
  18.4 7.8 %collective-permute-start.6 = (bf16[2,80,256]{2,1,0:T(8,128)(2,1)S(1)}, bf16[2,80,256]{2,1,0:T(8,128)(2,1)S(1)}, u32[]{:S(2)}, u32[]{:S(2)}) collective-permute-start(bf16[2,80,256]{2,1,0:T(8,128)(2,1)S(1)} %pad_maximum_fusion.1), channel_id=1, source_target_pairs={{0,64},{32,96},{64,128},{96,160},{128,192},{160,224},{192,0},{224,... | collective-permute-start | bytes 245768 | tf_op jit(solution)/shard_map/ppermute | solution.py:27
  26.3 0.7 copy-start.4
  28.7 19.9 %all-to-all-start = ((s32[64,1,16]{2,1,0:T(1,128)}), s32[64,1,16]{2,1,0:T(1,128)S(1)}, u32[]{:S(2)}, u32[]{:S(2)}) async-start(s32[64,1,16]{2,1,0:T(1,128)} %broadcast_in_dim.63), calls=%async_computation | async-start | bytes 65536 | tf_op jit(solution)/shard_map/all_to_all | solution.py:22
  53.3 15.2 %all-to-all-start.1 = ((s32[64,1,384]{2,1,0:T(1,128)}), s32[64,1,384]{2,1,0:T(1,128)S(1)}, u32[]{:S(2)}, u32[]{:S(2)}) async-start(s32[64,1,384]{2,1,0:T(1,128)} %copy.27), calls=%async_computation.1 | async-start | bytes 196608 | tf_op jit(solution)/shard_map/all_to_all | solution.py:22
  68.5 40.1 %copy-start.1 = (f32[1024]{0:T(1024)S(1)}, f32[1024]{0:T(1024)}, u32[]{:S(2)}) copy-start(f32[1024]{0:T(1024)} %param.24) | copy-start | bytes 12292
  68.5 40.1 %copy-start.2 = (f32[8]{0:T(128)S(1)}, f32[8]{0:T(128)}, u32[]{:S(2)}) copy-start(f32[8]{0:T(128)} %bias_ref.1) | copy-start | bytes 100
  83.3 25.3 %all-to-all-start.2 = ((bf16[4,512,256]{2,1,0:T(8,128)(2,1)}), bf16[4,512,256]{2,1,0:T(8,128)(2,1)S(1)}, u32[]{:S(2)}, u32[]{:S(2)}) async-start(bf16[4,512,256]{2,1,0:T(8,128)(2,1)} %bitcast.8), calls=%async_computation.2 | async-start | bytes 2097152 | tf_op jit(solution)/shard_map/all_to_all | solution.py:22
  87.7 17.8 %collective-permute-start.2 = (bf16[128,512]{1,0:T(8,128)(2,1)S(1)}, bf16[128,512]{1,0:T(8,128)(2,1)S(1)}, u32[]{:S(2)}, u32[]{:S(2)}) collective-permute-start(bf16[128,512]{1,0:T(8,128)(2,1)S(1)} %get-tuple-element.13), channel_id=1, source_target_pairs={{0,3},{1,0},{2,1},{3,2},{4,7},{5,4},{6,5},{7,6},{8,11},{9,8},{10,9... | collective-permute-start | bytes 393224 | tf_op jit(solution)/shard_map/ppermute | solution.py:27
  91.0 16.0 %collective-permute-start.1 = (bf16[128,512]{1,0:T(8,128)(2,1)S(1)}, bf16[128,512]{1,0:T(8,128)(2,1)S(1)}, u32[]{:S(2)}, u32[]{:S(2)}) collective-permute-start(bf16[128,512]{1,0:T(8,128)(2,1)S(1)} %get-tuple-element.14), channel_id=1, source_target_pairs={{0,2},{1,3},{2,0},{3,1},{4,6},{5,7},{6,4},{7,5},{8,10},{9,11},{10,... | collective-permute-start | bytes 393224 | tf_op jit(solution)/shard_map/ppermute | solution.py:27
  91.8 16.6 %collective-permute-start = (bf16[128,512]{1,0:T(8,128)(2,1)S(1)}, bf16[128,512]{1,0:T(8,128)(2,1)S(1)}, u32[]{:S(2)}, u32[]{:S(2)}) collective-permute-start(bf16[128,512]{1,0:T(8,128)(2,1)S(1)} %get-tuple-element.15), channel_id=1, source_target_pairs={{0,1},{1,2},{2,3},{3,0},{4,5},{5,6},{6,7},{7,4},{8,9},{9,10},{10,1... | collective-permute-start | bytes 393224 | tf_op jit(solution)/shard_map/ppermute | solution.py:27
  108.7 37.2 %copy-start.7 = (s32[8]{0:T(128)S(1)}, s32[8]{0:T(128)}, u32[]{:S(2)}) copy-start(s32[8]{0:T(128)} %param.21) | copy-start | bytes 100
  125.8 18.1 %all-to-all-start.3 = ((bf16[4,512,256]{2,1,0:T(8,128)(2,1)}), bf16[4,512,256]{2,1,0:T(8,128)(2,1)S(1)}, u32[]{:S(2)}, u32[]{:S(2)}) async-start(bf16[4,512,256]{2,1,0:T(8,128)(2,1)} %encoder.1), calls=%async_computation.3 | async-start | bytes 2097152 | tf_op jit(solution)/shard_map/all_to_all | solution.py:22
  143.9 8.4 %copy-start.3 = (bf16[4,512,256]{2,1,0:T(8,128)(2,1)}, bf16[4,512,256]{2,1,0:T(8,128)(2,1)S(1)}, u32[]{:S(2)}) copy-start(bf16[4,512,256]{2,1,0:T(8,128)(2,1)S(1)} %all-to-all-done.3) | copy-start | bytes 3145732
  143.9 8.4 %collective-permute-start.7 = (bf16[256,256]{1,0:T(8,128)(2,1)S(1)}, bf16[256,256]{1,0:T(8,128)(2,1)S(1)}, u32[]{:S(2)}, u32[]{:S(2)}) collective-permute-start(bf16[256,256]{1,0:T(8,128)(2,1)S(1)} %slice.39), channel_id=1, source_target_pairs={{0,4},{4,8},{8,12},{12,16},{16,20},{20,24},{24,28},{28,32},{32,36}... | collective-permute-start | bytes 393224 | tf_op jit(solution)/shard_map/ppermute | solution.py:356
  152.3 0.6 copy-start.5
Sparse Core Ops, SparseCore 0:
  27.1 64.8 all-gather.1

commit v2 on v1

--- a/solution.py
+++ b/solution.py
@@ -288,7 +288,7 @@
             cca_kv.reshape(rows_here, columns),
         ],
         axis=0,
-    )[None]
+    )
     share = doubled(share, "z", 4)
     share = jnp.concatenate([share] + [moved(share, "z", d) for d in TURNS[1:]], axis=0)
     wanted = exchange(request, SEQ)[:, 0]
@@ -300,14 +300,12 @@
         ],
         axis=1,
     )
-    reply, pieces_here = lax.optimization_barrier(
-        (reply, cond_kv.reshape(tp_size, my_tokens, 2 * columns))
-    )
+    pieces_here = cond_kv.reshape(tp_size, my_tokens, 2 * columns)
     fetched = exchange(reply, SEQ)
     z_count = lax.axis_size("z")
-    shares = lax.all_gather(
-        share.reshape(z_count * 5 * rows_here, columns), ("tp", "y", "core"), axis=0
-    ).reshape(tp_size, seq_size, 5 * rows_here, columns)
+    shares = lax.all_gather(share, ("tp", "y", "core"), axis=0).reshape(
+        tp_size, seq_size, 5 * rows_here, columns
+    )
     cond = jnp.stack(
         [lax.dynamic_index_in_dim(pieces_here, here, 0, keepdims=False)]
         + [

time: 166 us -> 167 us (level)
  local copies, waits for them, and re-layouts: 21.6 us -> 23.7 us
    unnamed x22 -> x25, local copies, waits for them, and re-layouts: 2.92 us -> 5.06 us
  transfers between devices with their start and end apart: 13 -> 13, of which waited for: 9 -> 8; matrix products, arithmetic and copies ran while one was open for 15% -> 15% of each run, Pallas kernels for 0% -> 0%
where the time goes in v2:
time: 167 us; the launch traced here: 166 us
  waiting for transfers between devices  56.7 us (34%)
  starting transfers between devices  43.8 us (26%)
  local copies, waits for them, and re-layouts  23.7 us (14%)
  Pallas kernels  22.6 us (14%)
  between operations  13.7 us (8%)
  matrix products  2.8 us (2%)
  other arithmetic  2.63 us (2%)
    all_to_all x4, waiting for transfers between devices, exchange(): return lax.all_to_all(value, axis, split_axis=0, concat_axis=0, tiled=True)  31.2 us
    all_to_all x4, starting transfers between devices, exchange(): return lax.all_to_all(value, axis, split_axis=0, concat_axis=0, tiled=True)  24.7 us
    ppermute x6, waiting for transfers between devices, moved(): lax.ppermute(value, axis, [(i, (i + steps) % count) for i in range(count)])  19.5 us
    pallas_call x1, Pallas kernels, encoder(): pl.pallas_call(functools.partial(encoder_body, parts, my_units, length, c...  17.1 us
    gather x1, local copies, waits for them, and re-layouts, parts(): jnp.take(table, tokens, axis=0).astype(jnp.float32)  11.2 us
    ppermute x6, starting transfers between devices, moved(): lax.ppermute(value, axis, [(i, (i + steps) % count) for i in range(count)])  10.9 us
    ppermute x1, starting transfers between devices, swapped(): return lax.ppermute(value, axis, [(i, i ^ distance) for i in range(count)])  6.29 us
    ppermute x1, waiting for transfers between devices, parts(): lax.ppermute(keys_values[(block_count - 1) * key_rows:], SEQ, [(s, s + 1)...  5.92 us
  transfers between devices with their start and end apart: 13, of which 8 were waited for; matrix products, arithmetic and copies ran while one was open for 15% of the time, Pallas kernels for 0%

profile of v2, /device:TPU:32, one launch (start us, length us, event | category | flops | bytes accessed | tf_op | source)
XLA Modules:
  0.0 166.0 jit_solution(1184547082640305294)
XLA Ops:
  6.5 0.0 copy-start
  6.5 0.0 all-gather.3.cloned.1.call-start
  6.5 0.7 copy.36
  7.3 0.8 pad_maximum_fusion.2
  8.0 6.3 %collective-permute-start.3 = (bf16[80,256]{1,0:T(8,128)(2,1)S(1)}, bf16[80,256]{1,0:T(8,128)(2,1)S(1)}, u32[]{:S(2)}, u32[]{:S(2)}) collective-permute-start(bf16[80,256]{1,0:T(8,128)(2,1)S(1)} %pad_maximum_fusion.2), channel_id=1, source_target_pairs={{0,128},{32,160},{64,192},{96,224},{128,0},{160,32},{192,64},{224,... | collective-permute-start | bytes 122888 | tf_op jit(solution)/shard_map/ppermute | solution.py:32
  14.3 0.7 constant_dynamic-update-slice_fusion.6
  15.1 0.7 constant_dynamic-update-slice_fusion.5
  15.8 0.7 constant_dynamic-update-slice_fusion.4
  16.5 0.0 collective-permute-done.3
  16.5 0.8 pad_maximum_fusion.1
  17.2 1.5 collective-permute-start.4
  18.7 0.5 collective-permute-start.5
  19.3 3.9 %collective-permute-start.6 = (bf16[160,256]{1,0:T(8,128)(2,1)S(1)}, bf16[160,256]{1,0:T(8,128)(2,1)S(1)}, u32[]{:S(2)}, u32[]{:S(2)}) collective-permute-start(bf16[160,256]{1,0:T(8,128)(2,1)S(1)} %pad_maximum_fusion.1), channel_id=1, source_target_pairs={{0,64},{32,96},{64,128},{96,160},{128,192},{160,224},{192,0},{224,... | collective-permute-start | bytes 245768 | tf_op jit(solution)/shard_map/ppermute | solution.py:27
  23.1 0.0 collective-permute-done.4
  23.1 0.0 collective-permute-done.5
  23.2 3.7 %collective-permute-done.6 = bf16[160,256]{1,0:T(8,128)(2,1)S(1)} collective-permute-done((bf16[160,256]{1,0:T(8,128)(2,1)S(1)}, bf16[160,256]{1,0:T(8,128)(2,1)S(1)}, u32[]{:S(2)}, u32[]{:S(2)}) %collective-permute-start.6) | collective-permute-done | bytes 81952 | tf_op jit(solution)/shard_map/ppermute | solution.py:27
  26.9 0.7 copy-done.4
  27.7 0.0 all-gather.3.cloned.1.call-update
  27.7 0.8 copy.26
  28.4 0.1 reshape.394
  28.6 0.1 select_reduce_fusion
  28.6 0.8 broadcast_in_dim.60
  29.4 11.3 %all-to-all-start = ((s32[64,1,16]{2,1,0:T(1,128)}), s32[64,1,16]{2,1,0:T(1,128)S(1)}, u32[]{:S(2)}, u32[]{:S(2)}) async-start(s32[64,1,16]{2,1,0:T(1,128)} %broadcast_in_dim.60), calls=%async_computation | async-start | bytes 65536 | tf_op jit(solution)/shard_map/all_to_all | solution.py:22
  40.7 0.1 reshape.395
  40.8 8.5 %all-to-all-done = s32[64,1,16]{2,1,0:T(1,128)S(1)} async-done(((s32[64,1,16]{2,1,0:T(1,128)}), s32[64,1,16]{2,1,0:T(1,128)S(1)}, u32[]{:S(2)}, u32[]{:S(2)}) %all-to-all-start) | async-done | bytes 4128 | tf_op jit(solution)/shard_map/all_to_all | solution.py:22
  49.3 0.1 slice_reduce_fusion
  49.4 0.0 copy-done
  49.5 0.6 gather_fusion.2
  50.1 1.5 gather_fusion.3
  51.6 1.5 gather_fusion.4
  53.2 0.1 broadcast_select_fusion.2
  53.2 0.7 copy.27
  54.0 5.5 %all-to-all-start.1 = ((s32[64,1,384]{2,1,0:T(1,128)}), s32[64,1,384]{2,1,0:T(1,128)S(1)}, u32[]{:S(2)}, u32[]{:S(2)}) async-start(s32[64,1,384]{2,1,0:T(1,128)} %copy.27), calls=%async_computation.1 | async-start | bytes 196608 | tf_op jit(solution)/shard_map/all_to_all | solution.py:22
  59.6 1.4 reshape.399
  61.0 8.2 %all-to-all-done.1 = s32[64,1,384]{2,1,0:T(1,128)S(1)} async-done(((s32[64,1,384]{2,1,0:T(1,128)}), s32[64,1,384]{2,1,0:T(1,128)S(1)}, u32[]{:S(2)}, u32[]{:S(2)}) %all-to-all-start.1) | async-done | bytes 98336 | tf_op jit(solution)/shard_map/all_to_all | solution.py:22
  69.2 0.0 copy-start.1
  69.2 0.0 copy-start.2
  69.2 0.6 gather_fusion
  69.8 0.1 broadcast_select_fusion.3
  69.9 11.2 %gather_fusion.1 = bf16[2048,256]{1,0:T(8,128)(2,1)S(1)} fusion(bf16[16384,256]{1,0:T(8,128)(2,1)} %param.22, s32[2048]{0:T(1024)S(1)} %broadcast_clamp_fusion), kind=kCustom, calls=%fused_computation.4 | custom fusion | bytes 2105344 | tf_op jit(solution)/shard_map/jit(_take)/gather | solution.py:328
  81.2 0.0 copy-done.6
  81.2 2.8 %fusion = bf16[2048,256]{1,0:T(8,128)(2,1)} fusion(bf16[32,256]{1,0:T(8,128)(2,1)S(1)} %copy-done.6, bf16[2048,256]{1,0:T(8,128)(2,1)S(1)} %gather_fusion.1, pred[2048]{0:T(1024)(128)(4,1)S(1)} %compare_and_fusion, s32[2048]{0:T(1024)S(1)} %get-tuple-element.13), kind=kOutput, calls=%fused_computation.6 | convolution fusion | flops 35717120 | bytes 2123776 | tf_op jit(solution)/shard_map/dot_general | solution.py:329
  84.0 4.3 %all-to-all-start.2 = ((bf16[4,512,256]{2,1,0:T(8,128)(2,1)}), bf16[4,512,256]{2,1,0:T(8,128)(2,1)S(1)}, u32[]{:S(2)}, u32[]{:S(2)}) async-start(bf16[4,512,256]{2,1,0:T(8,128)(2,1)} %bitcast.8), calls=%async_computation.2 | async-start | bytes 2097152 | tf_op jit(solution)/shard_map/all_to_all | solution.py:22
  88.3 3.3 %collective-permute-start.2 = (bf16[128,512]{1,0:T(8,128)(2,1)S(1)}, bf16[128,512]{1,0:T(8,128)(2,1)S(1)}, u32[]{:S(2)}, u32[]{:S(2)}) collective-permute-start(bf16[128,512]{1,0:T(8,128)(2,1)S(1)} %get-tuple-element.9), channel_id=1, source_target_pairs={{0,3},{1,0},{2,1},{3,2},{4,7},{5,4},{6,5},{7,6},{8,11},{9,8},{10,9... | collective-permute-start | bytes 393224 | tf_op jit(solution)/shard_map/ppermute | solution.py:27
  91.6 0.9 collective-permute-start.1
  92.5 0.9 collective-permute-start
  93.4 12.7 %collective-permute-done.2 = bf16[128,512]{1,0:T(8,128)(2,1)S(1)} collective-permute-done((bf16[128,512]{1,0:T(8,128)(2,1)S(1)}, bf16[128,512]{1,0:T(8,128)(2,1)S(1)}, u32[]{:S(2)}, u32[]{:S(2)}) %collective-permute-start.2) | collective-permute-done | bytes 131104 | tf_op jit(solution)/shard_map/ppermute | solution.py:27
  106.1 1.5 collective-permute-done.1
  107.7 1.4 collective-permute-done
  109.1 0.1 pad_maximum_fusion.cond_ref
  109.2 0.1 fusion.2.hit_ref
  109.3 0.0 all-to-all-done.2.emb_ref
  109.3 0.0 all-gather.3.cloned.1.call-done
  109.3 0.0 copy-done.1
  109.3 0.0 copy-done.2
  109.4 0.0 copy-start.7
  109.4 17.1 %encoder.1 = bf16[4,512,256]{2,1,0:T(8,128)(2,1)} custom-call(s32[1,64]{1,0:T(1,128)S(1)} %fusion.3.place_ref, s32[4]{0:T(128)S(1)} %and_select_fusion.3.xs_ref, f32[8]{0:T(128)S(1)} %copy-done.2, bf16[4,512,256]{2,1,0:T(8,128)(2,1)S(1)} %all-to-all-done.2.emb_ref, f32[1,1024]{1,0:T(1,128)S(1)} %bitcast.49, bf16[512,128]{1,0:T(8,128)(2,1)S(1)} %fusion.2.hit_ref, ...), custom_call_target="tpu_custom_call" | custom-call | tf_op jit(solution)/shard_map/encoder/pallas_call | solution.py:147
  126.5 3.5 %all-to-all-start.3 = ((bf16[4,512,256]{2,1,0:T(8,128)(2,1)}), bf16[4,512,256]{2,1,0:T(8,128)(2,1)S(1)}, u32[]{:S(2)}, u32[]{:S(2)}) async-start(bf16[4,512,256]{2,1,0:T(8,128)(2,1)} %encoder.1), calls=%async_computation.3 | async-start | bytes 2097152 | tf_op jit(solution)/shard_map/all_to_all | solution.py:22
  130.0 14.5 %all-to-all-done.3 = bf16[4,512,256]{2,1,0:T(8,128)(2,1)S(1)} async-done(((bf16[4,512,256]{2,1,0:T(8,128)(2,1)}), bf16[4,512,256]{2,1,0:T(8,128)(2,1)S(1)}, u32[]{:S(2)}, u32[]{:S(2)}) %all-to-all-start.3) | async-done | bytes 1048608 | tf_op jit(solution)/shard_map/all_to_all | solution.py:22
  144.6 1.9 %collective-permute-start.7 = (bf16[256,256]{1,0:T(8,128)(2,1)S(1)}, bf16[256,256]{1,0:T(8,128)(2,1)S(1)}, u32[]{:S(2)}, u32[]{:S(2)}) collective-permute-start(bf16[256,256]{1,0:T(8,128)(2,1)S(1)} %slice.39), channel_id=1, source_target_pairs={{0,4},{4,8},{8,12},{12,16},{16,20},{20,24},{24,28},{28,32},{32,36}... | collective-permute-start | bytes 393224 | tf_op jit(solution)/shard_map/ppermute | solution.py:354
  146.5 0.5 and_convert_fusion.allowed_ref
  147.1 5.9 %collective-permute-done.7.carried_ref = bf16[256,256]{1,0:T(8,128)(2,1)S(1)} collective-permute-done((bf16[256,256]{1,0:T(8,128)(2,1)S(1)}, bf16[256,256]{1,0:T(8,128)(2,1)S(1)}, u32[]{:S(2)}, u32[]{:S(2)}) %collective-permute-start.7) | collective-permute-done | bytes 131104 | tf_op jit(solution)/shard_map/ppermute | solution.py:354
  153.0 0.6 copy-done.5
  153.7 5.5 %attend.1 = bf16[512,1024]{1,0:T(8,128)(2,1)} custom-call(s32[8]{0:T(128)} %and_convert_fusion.allowed_ref, bf16[512,1024]{1,0:T(8,128)(2,1)} %q_ref.1, bf16[2048,256]{1,0:T(8,128)(2,1)} %bitcast.54, bf16[2048,256]{1,0:T(8,128)(2,1)} %bitcast.55, bf16[256,256]{1,0:T(8,128)(2,1)} %copy-done.5), custom_call_target="tpu_custom_call" | custom-call | tf_op jit(solution)/shard_map/attend/pallas_call | solution.py:228
  (28 shorter events, 0.2 us)
Async XLA Ops:
  6.5 42.9 %copy-start = (s32[512,128]{1,0:T(8,128)S(1)}, s32[512,128]{1,0:T(8,128)}, u32[]{:S(2)}) copy-start(s32[512,128]{1,0:T(8,128)} %param.17) | copy-start | bytes 786436
  6.5 74.6 %copy-start.6 = (bf16[32,256]{1,0:T(8,128)(2,1)S(1)}, bf16[32,256]{1,0:T(8,128)(2,1)}, u32[]{:S(2)}) copy-start(bf16[32,256]{1,0:T(8,128)(2,1)} %param.23) | copy-start | bytes 49156
  6.5 102.8 %all-gather.3.cloned.1.call-start = ((), (), s32[]{:S(2)}) async-start(), calls=%async_computation.4 | async-start | bytes 10813440 | tf_op jit(solution)/shard_map/all_gather | solution.py:306
  8.0 8.4 %collective-permute-start.3 = (bf16[80,256]{1,0:T(8,128)(2,1)S(1)}, bf16[80,256]{1,0:T(8,128)(2,1)S(1)}, u32[]{:S(2)}, u32[]{:S(2)}) collective-permute-start(bf16[80,256]{1,0:T(8,128)(2,1)S(1)} %pad_maximum_fusion.2), channel_id=1, source_target_pairs={{0,128},{32,160},{64,192},{96,224},{128,0},{160,32},{192,64},{224,... | collective-permute-start | bytes 122888 | tf_op jit(solution)/shard_map/ppermute | solution.py:32
  17.2 5.9 %collective-permute-start.4 = (bf16[160,256]{1,0:T(8,128)(2,1)S(1)}, bf16[160,256]{1,0:T(8,128)(2,1)S(1)}, u32[]{:S(2)}, u32[]{:S(2)}) collective-permute-start(bf16[160,256]{1,0:T(8,128)(2,1)S(1)} %pad_maximum_fusion.1), channel_id=1, source_target_pairs={{0,32},{32,64},{64,96},{96,128},{128,160},{160,192},{192,224},{224... | collective-permute-start | bytes 245768 | tf_op jit(solution)/shard_map/ppermute | solution.py:27
  18.7 4.4 %collective-permute-start.5 = (bf16[160,256]{1,0:T(8,128)(2,1)S(1)}, bf16[160,256]{1,0:T(8,128)(2,1)S(1)}, u32[]{:S(2)}, u32[]{:S(2)}) collective-permute-start(bf16[160,256]{1,0:T(8,128)(2,1)S(1)} %pad_maximum_fusion.1), channel_id=1, source_target_pairs={{0,224},{32,0},{64,32},{96,64},{128,96},{160,128},{192,160},{224,1... | collective-permute-start | bytes 245768 | tf_op jit(solution)/shard_map/ppermute | solution.py:27
  19.3 7.7 %collective-permute-start.6 = (bf16[160,256]{1,0:T(8,128)(2,1)S(1)}, bf16[160,256]{1,0:T(8,128)(2,1)S(1)}, u32[]{:S(2)}, u32[]{:S(2)}) collective-permute-start(bf16[160,256]{1,0:T(8,128)(2,1)S(1)} %pad_maximum_fusion.1), channel_id=1, source_target_pairs={{0,64},{32,96},{64,128},{96,160},{128,192},{160,224},{192,0},{224,... | collective-permute-start | bytes 245768 | tf_op jit(solution)/shard_map/ppermute | solution.py:27
  26.9 0.7 copy-start.4
  29.4 19.9 %all-to-all-start = ((s32[64,1,16]{2,1,0:T(1,128)}), s32[64,1,16]{2,1,0:T(1,128)S(1)}, u32[]{:S(2)}, u32[]{:S(2)}) async-start(s32[64,1,16]{2,1,0:T(1,128)} %broadcast_in_dim.60), calls=%async_computation | async-start | bytes 65536 | tf_op jit(solution)/shard_map/all_to_all | solution.py:22
  54.0 15.2 %all-to-all-start.1 = ((s32[64,1,384]{2,1,0:T(1,128)}), s32[64,1,384]{2,1,0:T(1,128)S(1)}, u32[]{:S(2)}, u32[]{:S(2)}) async-start(s32[64,1,384]{2,1,0:T(1,128)} %copy.27), calls=%async_computation.1 | async-start | bytes 196608 | tf_op jit(solution)/shard_map/all_to_all | solution.py:22
  69.2 40.1 %copy-start.1 = (f32[1024]{0:T(1024)S(1)}, f32[1024]{0:T(1024)}, u32[]{:S(2)}) copy-start(f32[1024]{0:T(1024)} %param.24) | copy-start | bytes 12292
  69.2 40.1 %copy-start.2 = (f32[8]{0:T(128)S(1)}, f32[8]{0:T(128)}, u32[]{:S(2)}) copy-start(f32[8]{0:T(128)} %bias_ref.1) | copy-start | bytes 100
  84.0 25.3 %all-to-all-start.2 = ((bf16[4,512,256]{2,1,0:T(8,128)(2,1)}), bf16[4,512,256]{2,1,0:T(8,128)(2,1)S(1)}, u32[]{:S(2)}, u32[]{:S(2)}) async-start(bf16[4,512,256]{2,1,0:T(8,128)(2,1)} %bitcast.8), calls=%async_computation.2 | async-start | bytes 2097152 | tf_op jit(solution)/shard_map/all_to_all | solution.py:22
  88.3 17.8 %collective-permute-start.2 = (bf16[128,512]{1,0:T(8,128)(2,1)S(1)}, bf16[128,512]{1,0:T(8,128)(2,1)S(1)}, u32[]{:S(2)}, u32[]{:S(2)}) collective-permute-start(bf16[128,512]{1,0:T(8,128)(2,1)S(1)} %get-tuple-element.9), channel_id=1, source_target_pairs={{0,3},{1,0},{2,1},{3,2},{4,7},{5,4},{6,5},{7,6},{8,11},{9,8},{10,9... | collective-permute-start | bytes 393224 | tf_op jit(solution)/shard_map/ppermute | solution.py:27
  91.6 16.0 %collective-permute-start.1 = (bf16[128,512]{1,0:T(8,128)(2,1)S(1)}, bf16[128,512]{1,0:T(8,128)(2,1)S(1)}, u32[]{:S(2)}, u32[]{:S(2)}) collective-permute-start(bf16[128,512]{1,0:T(8,128)(2,1)S(1)} %get-tuple-element.10), channel_id=1, source_target_pairs={{0,2},{1,3},{2,0},{3,1},{4,6},{5,7},{6,4},{7,5},{8,10},{9,11},{10,... | collective-permute-start | bytes 393224 | tf_op jit(solution)/shard_map/ppermute | solution.py:27
  92.5 16.6 %collective-permute-start = (bf16[128,512]{1,0:T(8,128)(2,1)S(1)}, bf16[128,512]{1,0:T(8,128)(2,1)S(1)}, u32[]{:S(2)}, u32[]{:S(2)}) collective-permute-start(bf16[128,512]{1,0:T(8,128)(2,1)S(1)} %get-tuple-element.11), channel_id=1, source_target_pairs={{0,1},{1,2},{2,3},{3,0},{4,5},{5,6},{6,7},{7,4},{8,9},{9,10},{10,1... | collective-permute-start | bytes 393224 | tf_op jit(solution)/shard_map/ppermute | solution.py:27
  109.4 37.2 %copy-start.7 = (s32[8]{0:T(128)S(1)}, s32[8]{0:T(128)}, u32[]{:S(2)}) copy-start(s32[8]{0:T(128)} %param.21) | copy-start | bytes 100
  126.5 18.1 %all-to-all-start.3 = ((bf16[4,512,256]{2,1,0:T(8,128)(2,1)}), bf16[4,512,256]{2,1,0:T(8,128)(2,1)S(1)}, u32[]{:S(2)}, u32[]{:S(2)}) async-start(bf16[4,512,256]{2,1,0:T(8,128)(2,1)} %encoder.1), calls=%async_computation.3 | async-start | bytes 2097152 | tf_op jit(solution)/shard_map/all_to_all | solution.py:22
  144.6 8.4 %copy-start.3 = (bf16[4,512,256]{2,1,0:T(8,128)(2,1)}, bf16[4,512,256]{2,1,0:T(8,128)(2,1)S(1)}, u32[]{:S(2)}) copy-start(bf16[4,512,256]{2,1,0:T(8,128)(2,1)S(1)} %all-to-all-done.3) | copy-start | bytes 3145732
  144.6 8.4 %collective-permute-start.7 = (bf16[256,256]{1,0:T(8,128)(2,1)S(1)}, bf16[256,256]{1,0:T(8,128)(2,1)S(1)}, u32[]{:S(2)}, u32[]{:S(2)}) collective-permute-start(bf16[256,256]{1,0:T(8,128)(2,1)S(1)} %slice.39), channel_id=1, source_target_pairs={{0,4},{4,8},{8,12},{12,16},{16,20},{20,24},{24,28},{28,32},{32,36}... | collective-permute-start | bytes 393224 | tf_op jit(solution)/shard_map/ppermute | solution.py:354
  153.0 0.6 copy-start.5
Sparse Core Ops, SparseCore 0:
  27.8 64.8 all-gather.2

commit v3 on v2

--- a/solution.py
+++ b/solution.py
@@ -290,6 +290,7 @@
         axis=0,
     )
     share = doubled(share, "z", 4)
+    share, request = lax.optimization_barrier((share, request))
     share = jnp.concatenate([share] + [moved(share, "z", d) for d in TURNS[1:]], axis=0)
     wanted = exchange(request, SEQ)[:, 0]
     reply = jnp.concatenate(
@@ -300,7 +301,9 @@
         ],
         axis=1,
     )
-    pieces_here = cond_kv.reshape(tp_size, my_tokens, 2 * columns)
+    reply, pieces_here = lax.optimization_barrier(
+        (reply, cond_kv.reshape(tp_size, my_tokens, 2 * columns))
+    )
     fetched = exchange(reply, SEQ)
     z_count = lax.axis_size("z")
     shares = lax.all_gather(share, ("tp", "y", "core"), axis=0).reshape(
@@ -317,6 +320,7 @@
             for d in range(1, tp_size)
         ]
     )
+    fetched, cond = lax.optimization_barrier((fetched, cond))
     fetched = jnp.take(fetched, holder, axis=0)
     tokens = fetched[:, :length].reshape(unit_count * length)
     depths = fetched[:, length : 2 * length].reshape(unit_count * length)

time: 167 us -> 164 us (0.982)
  local copies, waits for them, and re-layouts: 23.7 us -> 20.7 us
    ppermute x6, waiting for transfers between devices: 19.5 us -> 4.3 us  [moved(): lax.ppermute(value, axis, [(i, (i + steps) % count) for i in range(count)])]
    all_to_all x4, waiting for transfers between devices: 31.2 us -> 45.6 us  [exchange(): return lax.all_to_all(value, axis, split_axis=0, concat_axis=0, tiled=True)]
    unnamed x25 -> x17, local copies, waits for them, and re-layouts: 5.06 us -> 2.2 us
  transfers between devices with their start and end apart: 13 -> 13, of which waited for: 8 -> 10; matrix products, arithmetic and copies ran while one was open for 15% -> 14% of each run, Pallas kernels for 0% -> 0%
where the time goes in v3:
time: 164 us
  waiting for transfers between devices  56.8 us (35%)
  starting transfers between devices  43.5 us (27%)
  Pallas kernels  22.6 us (14%)
  local copies, waits for them, and re-layouts  20.7 us (13%)
  between operations  13.7 us (8%)
  other arithmetic  3.43 us (2%)
  matrix products  2.8 us (2%)
    all_to_all x4, waiting for transfers between devices, exchange(): return lax.all_to_all(value, axis, split_axis=0, concat_axis=0, tiled=True)  45.6 us
    all_to_all x4, starting transfers between devices, exchange(): return lax.all_to_all(value, axis, split_axis=0, concat_axis=0, tiled=True)  24.8 us
    pallas_call x1, Pallas kernels, encoder(): pl.pallas_call(functools.partial(encoder_body, parts, my_units, length, c...  17.1 us
    gather x1, local copies, waits for them, and re-layouts, parts(): jnp.take(table, tokens, axis=0).astype(jnp.float32)  11.1 us
    ppermute x6, starting transfers between devices, moved(): lax.ppermute(value, axis, [(i, (i + steps) % count) for i in range(count)])  10.6 us
    ppermute x1, starting transfers between devices, swapped(): return lax.ppermute(value, axis, [(i, i ^ distance) for i in range(count)])  6.29 us
    ppermute x1, waiting for transfers between devices, parts(): lax.ppermute(keys_values[(block_count - 1) * key_rows:], SEQ, [(s, s + 1)...  5.87 us
    pallas_call x1, Pallas kernels, attend(): pl.pallas_call(functools.partial(attend_body, heads, group), out_shape=ja...  5.49 us
  transfers between devices with their start and end apart: 13, of which 10 were waited for; matrix products, arithmetic and copies ran while one was open for 14% of the time, Pallas kernels for 0%

profile of v3, /device:TPU:32, one launch (start us, length us, event | category | flops | bytes accessed | tf_op | source)
XLA Modules:
  0.0 163.6 jit_solution(13100234714598751383)
XLA Ops:
  6.5 0.0 copy-start
  6.5 0.0 copy-start.5
  6.5 0.0 all-gather.3.cloned.1.call-start
  6.5 0.7 copy.34
  7.3 0.8 pad_maximum_fusion.3
  8.0 6.3 %collective-permute-start = (bf16[80,256]{1,0:T(8,128)(2,1)S(1)}, bf16[80,256]{1,0:T(8,128)(2,1)S(1)}, u32[]{:S(2)}, u32[]{:S(2)}) collective-permute-start(bf16[80,256]{1,0:T(8,128)(2,1)S(1)} %pad_maximum_fusion.3), channel_id=1, source_target_pairs={{0,128},{32,160},{64,192},{96,224},{128,0},{160,32},{192,64},{224,... | collective-permute-start | bytes 122888 | tf_op jit(solution)/shard_map/ppermute | solution.py:32
  14.3 0.8 copy.26
  15.1 0.1 reshape.391
  15.2 0.1 select_reduce_fusion
  15.3 1.0 collective-permute-done
  16.3 0.8 pad_maximum_fusion.2
  17.1 0.7 broadcast_in_dim.60
  17.8 2.9 %collective-permute-start.6 = (bf16[160,256]{1,0:T(8,128)(2,1)S(1)}, bf16[160,256]{1,0:T(8,128)(2,1)S(1)}, u32[]{:S(2)}, u32[]{:S(2)}) collective-permute-start(bf16[160,256]{1,0:T(8,128)(2,1)S(1)} %pad_maximum_fusion.2), channel_id=1, source_target_pairs={{0,64},{32,96},{64,128},{96,160},{128,192},{160,224},{192,0},{224,... | collective-permute-start | bytes 245768 | tf_op jit(solution)/shard_map/ppermute | solution.py:27
  20.7 0.2 collective-permute-start.5
  20.9 2.9 %collective-permute-start.4 = (bf16[160,256]{1,0:T(8,128)(2,1)S(1)}, bf16[160,256]{1,0:T(8,128)(2,1)S(1)}, u32[]{:S(2)}, u32[]{:S(2)}) collective-permute-start(bf16[160,256]{1,0:T(8,128)(2,1)S(1)} %pad_maximum_fusion.2), channel_id=1, source_target_pairs={{0,32},{32,64},{64,96},{96,128},{128,160},{160,192},{192,224},{224... | collective-permute-start | bytes 245768 | tf_op jit(solution)/shard_map/ppermute | solution.py:27
  23.8 1.9 %collective-permute-done.6 = bf16[160,256]{1,0:T(8,128)(2,1)S(1)} collective-permute-done((bf16[160,256]{1,0:T(8,128)(2,1)S(1)}, bf16[160,256]{1,0:T(8,128)(2,1)S(1)}, u32[]{:S(2)}, u32[]{:S(2)}) %collective-permute-start.6) | collective-permute-done | bytes 81952 | tf_op jit(solution)/shard_map/ppermute | solution.py:27
  25.7 0.5 collective-permute-done.5
  26.2 0.6 collective-permute-done.4
  26.8 0.8 pad_maximum_fusion.1
  27.6 0.0 all-gather.3.cloned.1.call-update
  27.6 12.0 %all-to-all-start = ((s32[64,1,16]{2,1,0:T(1,128)}), s32[64,1,16]{2,1,0:T(1,128)S(1)}, u32[]{:S(2)}, u32[]{:S(2)}) async-start(s32[64,1,16]{2,1,0:T(1,128)} %bitcast.5), calls=%async_computation | async-start | bytes 65536 | tf_op jit(solution)/shard_map/all_to_all | solution.py:22
  39.7 0.1 reshape.395
  39.7 1.4 reshape.394
  41.1 7.1 %all-to-all-done = s32[64,1,16]{2,1,0:T(1,128)S(1)} async-done(((s32[64,1,16]{2,1,0:T(1,128)}), s32[64,1,16]{2,1,0:T(1,128)S(1)}, u32[]{:S(2)}, u32[]{:S(2)}) %all-to-all-start) | async-done | bytes 4128 | tf_op jit(solution)/shard_map/all_to_all | solution.py:22
  48.2 0.1 slice_reduce_fusion
  48.3 0.0 copy-done
  48.3 0.6 gather_fusion.2
  48.9 1.6 gather_fusion.3
  50.5 1.5 gather_fusion.4
  52.1 0.1 broadcast_select_fusion.2
  52.1 0.1 constant_dynamic-slice_fusion
  52.2 0.0 copy-start.1
  52.2 0.0 copy-start.2
  52.2 2.8 %collective-permute-start.3 = (bf16[128,512]{1,0:T(8,128)(2,1)S(1)}, bf16[128,512]{1,0:T(8,128)(2,1)S(1)}, u32[]{:S(2)}, u32[]{:S(2)}) collective-permute-start(bf16[128,512]{1,0:T(8,128)(2,1)S(1)} %get-tuple-element.21), channel_id=1, source_target_pairs={{0,3},{1,0},{2,1},{3,2},{4,7},{5,4},{6,5},{7,6},{8,11},{9,8},{10,9... | collective-permute-start | bytes 393224 | tf_op jit(solution)/shard_map/ppermute | solution.py:27
  55.1 0.8 collective-permute-start.2
  55.9 0.9 collective-permute-start.1
  56.8 0.7 copy.27
  57.5 5.5 %all-to-all-start.1 = ((s32[64,1,384]{2,1,0:T(1,128)}), s32[64,1,384]{2,1,0:T(1,128)S(1)}, u32[]{:S(2)}, u32[]{:S(2)}) async-start(s32[64,1,384]{2,1,0:T(1,128)} %copy.27), calls=%async_computation.1 | async-start | bytes 196608 | tf_op jit(solution)/shard_map/all_to_all | solution.py:22
  63.1 0.0 collective-permute-done.3
  63.1 0.0 collective-permute-done.2
  63.1 1.3 collective-permute-done.1
  64.4 0.1 pad_maximum_fusion.cond_ref
  64.4 8.3 %all-to-all-done.1 = s32[64,1,384]{2,1,0:T(1,128)S(1)} async-done(((s32[64,1,384]{2,1,0:T(1,128)}), s32[64,1,384]{2,1,0:T(1,128)S(1)}, u32[]{:S(2)}, u32[]{:S(2)}) %all-to-all-start.1) | async-done | bytes 98336 | tf_op jit(solution)/shard_map/all_to_all | solution.py:22
  72.7 0.6 gather_fusion
  73.3 0.1 broadcast_select_fusion.3
  73.4 11.1 %gather_fusion.1 = bf16[2048,256]{1,0:T(8,128)(2,1)S(1)} fusion(bf16[16384,256]{1,0:T(8,128)(2,1)} %param.22, s32[2048]{0:T(1024)S(1)} %broadcast_clamp_fusion), kind=kCustom, calls=%fused_computation.4 | custom fusion | bytes 2105344 | tf_op jit(solution)/shard_map/jit(_take)/gather | solution.py:332
  84.5 0.0 copy-done.5
  84.5 2.8 %fusion = bf16[2048,256]{1,0:T(8,128)(2,1)} fusion(bf16[32,256]{1,0:T(8,128)(2,1)S(1)} %copy-done.5, bf16[2048,256]{1,0:T(8,128)(2,1)S(1)} %gather_fusion.1, pred[2048]{0:T(1024)(128)(4,1)S(1)} %compare_and_fusion, s32[2048]{0:T(1024)S(1)} %get-tuple-element.25), kind=kOutput, calls=%fused_computation.6 | convolution fusion | flops 35717120 | bytes 2123776 | tf_op jit(solution)/shard_map/dot_general | solution.py:333
  87.3 3.7 %all-to-all-start.2 = ((bf16[4,512,256]{2,1,0:T(8,128)(2,1)}), bf16[4,512,256]{2,1,0:T(8,128)(2,1)S(1)}, u32[]{:S(2)}, u32[]{:S(2)}) async-start(bf16[4,512,256]{2,1,0:T(8,128)(2,1)} %bitcast.19), calls=%async_computation.2 | async-start | bytes 2097152 | tf_op jit(solution)/shard_map/all_to_all | solution.py:22
  91.1 0.1 fusion.2.hit_ref
  91.3 15.4 %all-to-all-done.2.emb_ref = bf16[4,512,256]{2,1,0:T(8,128)(2,1)S(1)} async-done(((bf16[4,512,256]{2,1,0:T(8,128)(2,1)}), bf16[4,512,256]{2,1,0:T(8,128)(2,1)S(1)}, u32[]{:S(2)}, u32[]{:S(2)}) %all-to-all-start.2) | async-done | bytes 1048608 | tf_op jit(solution)/shard_map/all_to_all | solution.py:22
  106.7 0.0 all-gather.3.cloned.1.call-done
  106.7 0.0 copy-done.1
  106.7 0.0 copy-done.2
  106.7 17.1 %encoder.1 = bf16[4,512,256]{2,1,0:T(8,128)(2,1)} custom-call(s32[1,64]{1,0:T(1,128)S(1)} %fusion.3.place_ref, s32[4]{0:T(128)S(1)} %and_select_fusion.3.xs_ref, f32[8]{0:T(128)S(1)} %copy-done.2, bf16[4,512,256]{2,1,0:T(8,128)(2,1)S(1)} %all-to-all-done.2.emb_ref, f32[1,1024]{1,0:T(1,128)S(1)} %bitcast.46, bf16[512,128]{1,0:T(8,128)(2,1)S(1)} %fusion.2.hit_ref, ...), custom_call_target="tpu_custom_call" | custom-call | tf_op jit(solution)/shard_map/encoder/pallas_call | solution.py:147
  123.8 3.5 %all-to-all-start.3 = ((bf16[4,512,256]{2,1,0:T(8,128)(2,1)}), bf16[4,512,256]{2,1,0:T(8,128)(2,1)S(1)}, u32[]{:S(2)}, u32[]{:S(2)}) async-start(bf16[4,512,256]{2,1,0:T(8,128)(2,1)} %encoder.1), calls=%async_computation.3 | async-start | bytes 2097152 | tf_op jit(solution)/shard_map/all_to_all | solution.py:22
  127.4 14.8 %all-to-all-done.3 = bf16[4,512,256]{2,1,0:T(8,128)(2,1)S(1)} async-done(((bf16[4,512,256]{2,1,0:T(8,128)(2,1)}), bf16[4,512,256]{2,1,0:T(8,128)(2,1)S(1)}, u32[]{:S(2)}, u32[]{:S(2)}) %all-to-all-start.3) | async-done | bytes 1048608 | tf_op jit(solution)/shard_map/all_to_all | solution.py:22
  142.2 1.9 %collective-permute-start.7 = (bf16[256,256]{1,0:T(8,128)(2,1)S(1)}, bf16[256,256]{1,0:T(8,128)(2,1)S(1)}, u32[]{:S(2)}, u32[]{:S(2)}) collective-permute-start(bf16[256,256]{1,0:T(8,128)(2,1)S(1)} %slice.39), channel_id=1, source_target_pairs={{0,4},{4,8},{8,12},{12,16},{16,20},{20,24},{24,28},{28,32},{32,36}... | collective-permute-start | bytes 393224 | tf_op jit(solution)/shard_map/ppermute | solution.py:358
  144.2 0.0 copy-done.6
  144.2 0.6 and_convert_fusion.allowed_ref
  144.8 5.9 %collective-permute-done.7.carried_ref = bf16[256,256]{1,0:T(8,128)(2,1)S(1)} collective-permute-done((bf16[256,256]{1,0:T(8,128)(2,1)S(1)}, bf16[256,256]{1,0:T(8,128)(2,1)S(1)}, u32[]{:S(2)}, u32[]{:S(2)}) %collective-permute-start.7) | collective-permute-done | bytes 131104 | tf_op jit(solution)/shard_map/ppermute | solution.py:358
  150.6 0.0 copy-done.3
  150.6 0.7 copy-done.4
  151.3 5.5 %attend.1 = bf16[512,1024]{1,0:T(8,128)(2,1)} custom-call(s32[8]{0:T(128)} %and_convert_fusion.allowed_ref, bf16[512,1024]{1,0:T(8,128)(2,1)} %q_ref.1, bf16[2048,256]{1,0:T(8,128)(2,1)} %bitcast.51, bf16[2048,256]{1,0:T(8,128)(2,1)} %bitcast.52, bf16[256,256]{1,0:T(8,128)(2,1)} %copy-done.4), custom_call_target="tpu_custom_call" | custom-call | tf_op jit(solution)/shard_map/attend/pallas_call | solution.py:228
  (20 shorter events, 0.2 us)
Async XLA Ops:
  6.5 41.8 %copy-start = (s32[512,128]{1,0:T(8,128)S(1)}, s32[512,128]{1,0:T(8,128)}, u32[]{:S(2)}) copy-start(s32[512,128]{1,0:T(8,128)} %param.17) | copy-start | bytes 786436
  6.5 78.0 %copy-start.5 = (bf16[32,256]{1,0:T(8,128)(2,1)S(1)}, bf16[32,256]{1,0:T(8,128)(2,1)}, u32[]{:S(2)}) copy-start(bf16[32,256]{1,0:T(8,128)(2,1)} %param.23) | copy-start | bytes 49156
  6.5 100.2 %all-gather.3.cloned.1.call-start = ((), (), s32[]{:S(2)}) async-start(), calls=%async_computation.4 | async-start | bytes 10813440 | tf_op jit(solution)/shard_map/all_gather | solution.py:309
  8.0 8.3 %collective-permute-start = (bf16[80,256]{1,0:T(8,128)(2,1)S(1)}, bf16[80,256]{1,0:T(8,128)(2,1)S(1)}, u32[]{:S(2)}, u32[]{:S(2)}) collective-permute-start(bf16[80,256]{1,0:T(8,128)(2,1)S(1)} %pad_maximum_fusion.3), channel_id=1, source_target_pairs={{0,128},{32,160},{64,192},{96,224},{128,0},{160,32},{192,64},{224,... | collective-permute-start | bytes 122888 | tf_op jit(solution)/shard_map/ppermute | solution.py:32
  17.8 8.0 %collective-permute-start.6 = (bf16[160,256]{1,0:T(8,128)(2,1)S(1)}, bf16[160,256]{1,0:T(8,128)(2,1)S(1)}, u32[]{:S(2)}, u32[]{:S(2)}) collective-permute-start(bf16[160,256]{1,0:T(8,128)(2,1)S(1)} %pad_maximum_fusion.2), channel_id=1, source_target_pairs={{0,64},{32,96},{64,128},{96,160},{128,192},{160,224},{192,0},{224,... | collective-permute-start | bytes 245768 | tf_op jit(solution)/shard_map/ppermute | solution.py:27
  20.7 5.5 %collective-permute-start.5 = (bf16[160,256]{1,0:T(8,128)(2,1)S(1)}, bf16[160,256]{1,0:T(8,128)(2,1)S(1)}, u32[]{:S(2)}, u32[]{:S(2)}) collective-permute-start(bf16[160,256]{1,0:T(8,128)(2,1)S(1)} %pad_maximum_fusion.2), channel_id=1, source_target_pairs={{0,224},{32,0},{64,32},{96,64},{128,96},{160,128},{192,160},{224,1... | collective-permute-start | bytes 245768 | tf_op jit(solution)/shard_map/ppermute | solution.py:27
  20.9 5.9 %collective-permute-start.4 = (bf16[160,256]{1,0:T(8,128)(2,1)S(1)}, bf16[160,256]{1,0:T(8,128)(2,1)S(1)}, u32[]{:S(2)}, u32[]{:S(2)}) collective-permute-start(bf16[160,256]{1,0:T(8,128)(2,1)S(1)} %pad_maximum_fusion.2), channel_id=1, source_target_pairs={{0,32},{32,64},{64,96},{96,128},{128,160},{160,192},{192,224},{224... | collective-permute-start | bytes 245768 | tf_op jit(solution)/shard_map/ppermute | solution.py:27
  27.6 20.6 %all-to-all-start = ((s32[64,1,16]{2,1,0:T(1,128)}), s32[64,1,16]{2,1,0:T(1,128)S(1)}, u32[]{:S(2)}, u32[]{:S(2)}) async-start(s32[64,1,16]{2,1,0:T(1,128)} %bitcast.5), calls=%async_computation | async-start | bytes 65536 | tf_op jit(solution)/shard_map/all_to_all | solution.py:22
  52.2 54.5 %copy-start.1 = (f32[1024]{0:T(1024)S(1)}, f32[1024]{0:T(1024)}, u32[]{:S(2)}) copy-start(f32[1024]{0:T(1024)} %param.24) | copy-start | bytes 12292
  52.2 54.5 %copy-start.2 = (f32[8]{0:T(128)S(1)}, f32[8]{0:T(128)}, u32[]{:S(2)}) copy-start(f32[8]{0:T(128)} %bias_ref.1) | copy-start | bytes 100
  52.2 10.8 %collective-permute-start.3 = (bf16[128,512]{1,0:T(8,128)(2,1)S(1)}, bf16[128,512]{1,0:T(8,128)(2,1)S(1)}, u32[]{:S(2)}, u32[]{:S(2)}) collective-permute-start(bf16[128,512]{1,0:T(8,128)(2,1)S(1)} %get-tuple-element.21), channel_id=1, source_target_pairs={{0,3},{1,0},{2,1},{3,2},{4,7},{5,4},{6,5},{7,6},{8,11},{9,8},{10,9... | collective-permute-start | bytes 393224 | tf_op jit(solution)/shard_map/ppermute | solution.py:27
  55.1 8.0 %collective-permute-start.2 = (bf16[128,512]{1,0:T(8,128)(2,1)S(1)}, bf16[128,512]{1,0:T(8,128)(2,1)S(1)}, u32[]{:S(2)}, u32[]{:S(2)}) collective-permute-start(bf16[128,512]{1,0:T(8,128)(2,1)S(1)} %get-tuple-element.22), channel_id=1, source_target_pairs={{0,2},{1,3},{2,0},{3,1},{4,6},{5,7},{6,4},{7,5},{8,10},{9,11},{10,... | collective-permute-start | bytes 393224 | tf_op jit(solution)/shard_map/ppermute | solution.py:27
  55.9 8.5 %collective-permute-start.1 = (bf16[128,512]{1,0:T(8,128)(2,1)S(1)}, bf16[128,512]{1,0:T(8,128)(2,1)S(1)}, u32[]{:S(2)}, u32[]{:S(2)}) collective-permute-start(bf16[128,512]{1,0:T(8,128)(2,1)S(1)} %get-tuple-element.23), channel_id=1, source_target_pairs={{0,1},{1,2},{2,3},{3,0},{4,5},{5,6},{6,7},{7,4},{8,9},{9,10},{10,1... | collective-permute-start | bytes 393224 | tf_op jit(solution)/shard_map/ppermute | solution.py:27
  57.5 15.2 %all-to-all-start.1 = ((s32[64,1,384]{2,1,0:T(1,128)}), s32[64,1,384]{2,1,0:T(1,128)S(1)}, u32[]{:S(2)}, u32[]{:S(2)}) async-start(s32[64,1,384]{2,1,0:T(1,128)} %copy.27), calls=%async_computation.1 | async-start | bytes 196608 | tf_op jit(solution)/shard_map/all_to_all | solution.py:22
  87.3 19.4 %all-to-all-start.2 = ((bf16[4,512,256]{2,1,0:T(8,128)(2,1)}), bf16[4,512,256]{2,1,0:T(8,128)(2,1)S(1)}, u32[]{:S(2)}, u32[]{:S(2)}) async-start(bf16[4,512,256]{2,1,0:T(8,128)(2,1)} %bitcast.19), calls=%async_computation.2 | async-start | bytes 2097152 | tf_op jit(solution)/shard_map/all_to_all | solution.py:22
  106.7 37.5 %copy-start.6 = (s32[8]{0:T(128)S(1)}, s32[8]{0:T(128)}, u32[]{:S(2)}) copy-start(s32[8]{0:T(128)} %param.21) | copy-start | bytes 100
  123.8 18.4 %all-to-all-start.3 = ((bf16[4,512,256]{2,1,0:T(8,128)(2,1)}), bf16[4,512,256]{2,1,0:T(8,128)(2,1)S(1)}, u32[]{:S(2)}, u32[]{:S(2)}) async-start(bf16[4,512,256]{2,1,0:T(8,128)(2,1)} %encoder.1), calls=%async_computation.3 | async-start | bytes 2097152 | tf_op jit(solution)/shard_map/all_to_all | solution.py:22
  142.2 8.4 %copy-start.3 = (bf16[4,512,256]{2,1,0:T(8,128)(2,1)}, bf16[4,512,256]{2,1,0:T(8,128)(2,1)S(1)}, u32[]{:S(2)}) copy-start(bf16[4,512,256]{2,1,0:T(8,128)(2,1)S(1)} %all-to-all-done.3) | copy-start | bytes 3145732
  142.2 8.4 %collective-permute-start.7 = (bf16[256,256]{1,0:T(8,128)(2,1)S(1)}, bf16[256,256]{1,0:T(8,128)(2,1)S(1)}, u32[]{:S(2)}, u32[]{:S(2)}) collective-permute-start(bf16[256,256]{1,0:T(8,128)(2,1)S(1)} %slice.39), channel_id=1, source_target_pairs={{0,4},{4,8},{8,12},{12,16},{16,20},{20,24},{24,28},{28,32},{32,36}... | collective-permute-start | bytes 393224 | tf_op jit(solution)/shard_map/ppermute | solution.py:358
  150.6 0.7 copy-start.4
Sparse Core Ops, SparseCore 0:
  27.7 68.9 all-gather.2

commit v4 on v3

--- a/solution.py
+++ b/solution.py
@@ -293,14 +293,8 @@
     share, request = lax.optimization_barrier((share, request))
     share = jnp.concatenate([share] + [moved(share, "z", d) for d in TURNS[1:]], axis=0)
     wanted = exchange(request, SEQ)[:, 0]
-    reply = jnp.concatenate(
-        [
-            jnp.take(db_tokens, wanted, axis=0),
-            jnp.take(db_depth, wanted, axis=0),
-            jnp.take(db_parent, wanted, axis=0),
-        ],
-        axis=1,
-    )
+    stacked = jnp.concatenate([db_tokens, db_depth, db_parent], axis=1)
+    reply = jnp.take(stacked, wanted, axis=0, mode="clip")
     reply, pieces_here = lax.optimization_barrier(
         (reply, cond_kv.reshape(tp_size, my_tokens, 2 * columns))
     )
@@ -320,8 +314,7 @@
             for d in range(1, tp_size)
         ]
     )
-    fetched, cond = lax.optimization_barrier((fetched, cond))
-    fetched = jnp.take(fetched, holder, axis=0)
+    fetched = jnp.take(fetched, holder, axis=0, mode="clip")
     tokens = fetched[:, :length].reshape(unit_count * length)
     depths = fetched[:, length : 2 * length].reshape(unit_count * length)
     parents = fetched[:, 2 * length :]
@@ -329,7 +322,7 @@
         depths[:, None] == jnp.arange(depth_table.shape[0], dtype=jnp.int32)[None, :]
     ).astype(jnp.bfloat16)
     embedded = (
-        jnp.take(table, tokens, axis=0).astype(jnp.float32)
+        jnp.take(table, tokens, axis=0, mode="clip").astype(jnp.float32)
         + jnp.dot(depth_hit, depth_table, preferred_element_type=jnp.float32)
     ).astype(jnp.bfloat16)
     pieces = exchange(embedded.reshape(tp_size, my_units * length, columns), "tp")

time: 164 us -> 168 us (1.024); the launches traced: 164 us -> 166 us
  waiting for transfers between devices: 56.8 us -> 60.4 us
  local copies, waits for them, and re-layouts: 20.7 us -> 18.5 us
    ppermute x6, waiting for transfers between devices: 4.3 us -> 22.6 us  [moved(): lax.ppermute(value, axis, [(i, (i + steps) % count) for i in range(count)])]
    all_to_all x4, waiting for transfers between devices: 45.6 us -> 30.8 us  [exchange(): return lax.all_to_all(value, axis, split_axis=0, concat_axis=0, tiled=True)]
    gather x5 -> x3, local copies, waits for them, and re-layouts: 15.4 us -> 13.2 us  [the longest x1 12 us: parts(): jnp.take(table, tokens, axis=0, mode='clip').astype(jnp.float32)]
  transfers between devices with their start and end apart: 13 -> 13, of which waited for: 10 -> 11; matrix products, arithmetic and copies ran while one was open for 14% -> 12% of each run, Pallas kernels for 0% -> 0%
where the time goes in v4:
time: 168 us; the launch traced here: 166 us
  waiting for transfers between devices  60.4 us (36%)
  starting transfers between devices  44.8 us (27%)
  Pallas kernels  22.6 us (13%)
  local copies, waits for them, and re-layouts  18.5 us (11%)
  between operations  13.7 us (8%)
  other arithmetic  4.3 us (3%)
    all_to_all x4, waiting for transfers between devices, exchange(): return lax.all_to_all(value, axis, split_axis=0, concat_axis=0, tiled=True)  30.8 us
    all_to_all x4, starting transfers between devices, exchange(): return lax.all_to_all(value, axis, split_axis=0, concat_axis=0, tiled=True)  25.5 us
    ppermute x6, waiting for transfers between devices, moved(): lax.ppermute(value, axis, [(i, (i + steps) % count) for i in range(count)])  22.6 us
    pallas_call x1, Pallas kernels, encoder(): pl.pallas_call(functools.partial(encoder_body, parts, my_units, length, c...  17.1 us
    gather x1, local copies, waits for them, and re-layouts, parts(): jnp.take(table, tokens, axis=0, mode='clip').astype(jnp.float32)  12 us
    ppermute x6, starting transfers between devices, moved(): lax.ppermute(value, axis, [(i, (i + steps) % count) for i in range(count)])  11.1 us
    ppermute x1, starting transfers between devices, swapped(): return lax.ppermute(value, axis, [(i, i ^ distance) for i in range(count)])  6.29 us
    ppermute x1, waiting for transfers between devices, parts(): lax.ppermute(keys_values[(block_count - 1) * key_rows:], SEQ, [(s, s + 1)...  5.95 us
  transfers between devices with their start and end apart: 13, of which 11 were waited for; matrix products, arithmetic and copies ran while one was open for 12% of the time, Pallas kernels for 0%

profile of v4, /device:TPU:32, one launch (start us, length us, event | category | flops | bytes accessed | tf_op | source)
XLA Modules:
  0.0 165.8 jit_solution(13778877470049332082)
XLA Ops:
  6.5 0.0 copy-start
  6.5 0.0 all-gather.3.cloned.1.call-start
  6.5 0.7 copy.34
  7.3 0.8 pad_maximum_fusion.3
  8.0 6.3 %collective-permute-start = (bf16[80,256]{1,0:T(8,128)(2,1)S(1)}, bf16[80,256]{1,0:T(8,128)(2,1)S(1)}, u32[]{:S(2)}, u32[]{:S(2)}) collective-permute-start(bf16[80,256]{1,0:T(8,128)(2,1)S(1)} %pad_maximum_fusion.3), channel_id=1, source_target_pairs={{0,128},{32,160},{64,192},{96,224},{128,0},{160,32},{192,64},{224,... | collective-permute-start | bytes 122888 | tf_op jit(solution)/shard_map/ppermute | solution.py:32
  14.3 0.8 copy.26
  15.1 0.1 reshape.336
  15.1 0.1 select_reduce_fusion
  15.2 1.0 collective-permute-done
  16.3 0.8 pad_maximum_fusion.2
  17.0 0.7 broadcast_in_dim.38
  17.7 2.9 %collective-permute-start.6 = (bf16[160,256]{1,0:T(8,128)(2,1)S(1)}, bf16[160,256]{1,0:T(8,128)(2,1)S(1)}, u32[]{:S(2)}, u32[]{:S(2)}) collective-permute-start(bf16[160,256]{1,0:T(8,128)(2,1)S(1)} %pad_maximum_fusion.2), channel_id=1, source_target_pairs={{0,64},{32,96},{64,128},{96,160},{128,192},{160,224},{192,0},{224,... | collective-permute-start | bytes 245768 | tf_op jit(solution)/shard_map/ppermute | solution.py:27
  20.6 0.2 collective-permute-start.5
  20.9 2.9 %collective-permute-start.4 = (bf16[160,256]{1,0:T(8,128)(2,1)S(1)}, bf16[160,256]{1,0:T(8,128)(2,1)S(1)}, u32[]{:S(2)}, u32[]{:S(2)}) collective-permute-start(bf16[160,256]{1,0:T(8,128)(2,1)S(1)} %pad_maximum_fusion.2), channel_id=1, source_target_pairs={{0,32},{32,64},{64,96},{96,128},{128,160},{160,192},{192,224},{224... | collective-permute-start | bytes 245768 | tf_op jit(solution)/shard_map/ppermute | solution.py:27
  23.8 1.9 %collective-permute-done.6 = bf16[160,256]{1,0:T(8,128)(2,1)S(1)} collective-permute-done((bf16[160,256]{1,0:T(8,128)(2,1)S(1)}, bf16[160,256]{1,0:T(8,128)(2,1)S(1)}, u32[]{:S(2)}, u32[]{:S(2)}) %collective-permute-start.6) | collective-permute-done | bytes 81952 | tf_op jit(solution)/shard_map/ppermute | solution.py:27
  25.7 0.5 collective-permute-done.5
  26.2 0.6 collective-permute-done.4
  26.8 0.7 pad_maximum_fusion.1
  27.5 0.0 all-gather.3.cloned.1.call-update
  27.5 12.0 %all-to-all-start = ((s32[64,1,16]{2,1,0:T(1,128)}), s32[64,1,16]{2,1,0:T(1,128)S(1)}, u32[]{:S(2)}, u32[]{:S(2)}) async-start(s32[64,1,16]{2,1,0:T(1,128)} %bitcast.5), calls=%async_computation | async-start | bytes 65536 | tf_op jit(solution)/shard_map/all_to_all | solution.py:22
  39.6 1.2 pad_add_fusion
  40.7 0.1 reshape.338
  40.8 1.4 reshape.337
  42.2 6.0 %all-to-all-done = s32[64,1,16]{2,1,0:T(1,128)S(1)} async-done(((s32[64,1,16]{2,1,0:T(1,128)}), s32[64,1,16]{2,1,0:T(1,128)S(1)}, u32[]{:S(2)}, u32[]{:S(2)}) %all-to-all-start) | async-done | bytes 4128 | tf_op jit(solution)/shard_map/all_to_all | solution.py:22
  48.2 0.1 slice_reduce_fusion
  48.3 0.7 gather_fusion
  48.9 0.7 copy.27
  49.7 0.0 copy-start.1
  49.7 0.0 copy-start.2
  49.7 5.7 %all-to-all-start.1 = ((s32[64,1,384]{2,1,0:T(1,128)}), s32[64,1,384]{2,1,0:T(1,128)S(1)}, u32[]{:S(2)}, u32[]{:S(2)}) async-start(s32[64,1,384]{2,1,0:T(1,128)} %copy.27), calls=%async_computation.1 | async-start | bytes 196608 | tf_op jit(solution)/shard_map/all_to_all | solution.py:22
  55.4 9.6 %all-to-all-done.1 = s32[64,1,384]{2,1,0:T(1,128)S(1)} async-done(((s32[64,1,384]{2,1,0:T(1,128)}), s32[64,1,384]{2,1,0:T(1,128)S(1)}, u32[]{:S(2)}, u32[]{:S(2)}) %all-to-all-start.1) | async-done | bytes 98336 | tf_op jit(solution)/shard_map/all_to_all | solution.py:22
  65.0 0.6 gather_fusion.1
  65.6 12.0 %gather_fusion.2 = bf16[2048,256]{1,0:T(8,128)(2,1)S(1)} fusion(bf16[16384,256]{1,0:T(8,128)(2,1)} %param.20, s32[2048]{0:T(1024)S(1)} %fusion.3), kind=kCustom, calls=%fused_computation.2 | custom fusion | bytes 2105344 | tf_op jit(solution)/shard_map/jit(_take)/gather | solution.py:325
  77.6 0.0 copy-done
  77.6 1.5 fusion
  79.2 4.3 %all-to-all-start.2 = ((bf16[4,512,256]{2,1,0:T(8,128)(2,1)}), bf16[4,512,256]{2,1,0:T(8,128)(2,1)S(1)}, u32[]{:S(2)}, u32[]{:S(2)}) async-start(bf16[4,512,256]{2,1,0:T(8,128)(2,1)} %bitcast.11), calls=%async_computation.2 | async-start | bytes 2097152 | tf_op jit(solution)/shard_map/all_to_all | solution.py:22
  83.5 3.3 %collective-permute-start.3 = (bf16[128,512]{1,0:T(8,128)(2,1)S(1)}, bf16[128,512]{1,0:T(8,128)(2,1)S(1)}, u32[]{:S(2)}, u32[]{:S(2)}) collective-permute-start(bf16[128,512]{1,0:T(8,128)(2,1)S(1)} %get-tuple-element.14), channel_id=1, source_target_pairs={{0,3},{1,0},{2,1},{3,2},{4,7},{5,4},{6,5},{7,6},{8,11},{9,8},{10,9... | collective-permute-start | bytes 393224 | tf_op jit(solution)/shard_map/ppermute | solution.py:27
  86.8 0.9 collective-permute-start.2
  87.7 0.9 collective-permute-start.1
  88.5 15.9 %collective-permute-done.3 = bf16[128,512]{1,0:T(8,128)(2,1)S(1)} collective-permute-done((bf16[128,512]{1,0:T(8,128)(2,1)S(1)}, bf16[128,512]{1,0:T(8,128)(2,1)S(1)}, u32[]{:S(2)}, u32[]{:S(2)}) %collective-permute-start.3) | collective-permute-done | bytes 131104 | tf_op jit(solution)/shard_map/ppermute | solution.py:27
  104.5 1.5 collective-permute-done.2
  106.0 2.1 %collective-permute-done.1 = bf16[128,512]{1,0:T(8,128)(2,1)S(1)} collective-permute-done((bf16[128,512]{1,0:T(8,128)(2,1)S(1)}, bf16[128,512]{1,0:T(8,128)(2,1)S(1)}, u32[]{:S(2)}, u32[]{:S(2)}) %collective-permute-start.1) | collective-permute-done | bytes 131104 | tf_op jit(solution)/shard_map/ppermute | solution.py:27
  108.1 0.1 pad_maximum_fusion.cond_ref
  108.2 0.1 fusion.2.hit_ref
  108.4 0.0 all-to-all-done.2.emb_ref
  108.4 0.0 all-gather.3.cloned.1.call-done
  108.4 0.0 copy-done.1
  108.4 0.0 copy-done.2
  108.4 0.0 copy-start.5
  108.4 17.1 %encoder.1 = bf16[4,512,256]{2,1,0:T(8,128)(2,1)} custom-call(s32[1,64]{1,0:T(1,128)S(1)} %fusion.4.place_ref, s32[4]{0:T(128)S(1)} %and_select_fusion.3.xs_ref, f32[8]{0:T(128)S(1)} %copy-done.2, bf16[4,512,256]{2,1,0:T(8,128)(2,1)S(1)} %all-to-all-done.2.emb_ref, f32[1,1024]{1,0:T(1,128)S(1)} %bitcast.44, bf16[512,128]{1,0:T(8,128)(2,1)S(1)} %fusion.2.hit_ref, ...), custom_call_target="tpu_custom_call" | custom-call | tf_op jit(solution)/shard_map/encoder/pallas_call | solution.py:147
  125.6 3.5 %all-to-all-start.3 = ((bf16[4,512,256]{2,1,0:T(8,128)(2,1)}), bf16[4,512,256]{2,1,0:T(8,128)(2,1)S(1)}, u32[]{:S(2)}, u32[]{:S(2)}) async-start(bf16[4,512,256]{2,1,0:T(8,128)(2,1)} %encoder.1), calls=%async_computation.3 | async-start | bytes 2097152 | tf_op jit(solution)/shard_map/all_to_all | solution.py:22
  129.1 15.3 %all-to-all-done.3 = bf16[4,512,256]{2,1,0:T(8,128)(2,1)S(1)} async-done(((bf16[4,512,256]{2,1,0:T(8,128)(2,1)}), bf16[4,512,256]{2,1,0:T(8,128)(2,1)S(1)}, u32[]{:S(2)}, u32[]{:S(2)}) %all-to-all-start.3) | async-done | bytes 1048608 | tf_op jit(solution)/shard_map/all_to_all | solution.py:22
  144.4 0.0 copy-start.3
  144.4 1.9 %collective-permute-start.7 = (bf16[256,256]{1,0:T(8,128)(2,1)S(1)}, bf16[256,256]{1,0:T(8,128)(2,1)S(1)}, u32[]{:S(2)}, u32[]{:S(2)}) collective-permute-start(bf16[256,256]{1,0:T(8,128)(2,1)S(1)} %slice.35), channel_id=1, source_target_pairs={{0,4},{4,8},{8,12},{12,16},{16,20},{20,24},{24,28},{28,32},{32,36}... | collective-permute-start | bytes 393224 | tf_op jit(solution)/shard_map/ppermute | solution.py:351
  146.3 0.0 copy-done.5
  146.3 0.5 and_convert_fusion.allowed_ref
  146.9 5.9 %collective-permute-done.7.carried_ref = bf16[256,256]{1,0:T(8,128)(2,1)S(1)} collective-permute-done((bf16[256,256]{1,0:T(8,128)(2,1)S(1)}, bf16[256,256]{1,0:T(8,128)(2,1)S(1)}, u32[]{:S(2)}, u32[]{:S(2)}) %collective-permute-start.7) | collective-permute-done | bytes 131104 | tf_op jit(solution)/shard_map/ppermute | solution.py:351
  152.8 0.0 copy-done.3
  152.8 0.0 copy-start.4
  152.8 0.7 copy-done.4
  153.5 5.5 %attend.1 = bf16[512,1024]{1,0:T(8,128)(2,1)} custom-call(s32[8]{0:T(128)} %and_convert_fusion.allowed_ref, bf16[512,1024]{1,0:T(8,128)(2,1)} %q_ref.1, bf16[2048,256]{1,0:T(8,128)(2,1)} %bitcast.49, bf16[2048,256]{1,0:T(8,128)(2,1)} %bitcast.50, bf16[256,256]{1,0:T(8,128)(2,1)} %copy-done.4), custom_call_target="tpu_custom_call" | custom-call | tf_op jit(solution)/shard_map/attend/pallas_call | solution.py:228
  (12 shorter events, 0.1 us)
Async XLA Ops:
  6.5 71.1 %copy-start = (bf16[32,256]{1,0:T(8,128)(2,1)S(1)}, bf16[32,256]{1,0:T(8,128)(2,1)}, u32[]{:S(2)}) copy-start(bf16[32,256]{1,0:T(8,128)(2,1)} %param.21) | copy-start | bytes 49156
  6.5 101.9 %all-gather.3.cloned.1.call-start = ((), (), s32[]{:S(2)}) async-start(), calls=%async_computation.4 | async-start | bytes 10813440 | tf_op jit(solution)/shard_map/all_gather | solution.py:303
  8.0 8.3 %collective-permute-start = (bf16[80,256]{1,0:T(8,128)(2,1)S(1)}, bf16[80,256]{1,0:T(8,128)(2,1)S(1)}, u32[]{:S(2)}, u32[]{:S(2)}) collective-permute-start(bf16[80,256]{1,0:T(8,128)(2,1)S(1)} %pad_maximum_fusion.3), channel_id=1, source_target_pairs={{0,128},{32,160},{64,192},{96,224},{128,0},{160,32},{192,64},{224,... | collective-permute-start | bytes 122888 | tf_op jit(solution)/shard_map/ppermute | solution.py:32
  17.7 8.0 %collective-permute-start.6 = (bf16[160,256]{1,0:T(8,128)(2,1)S(1)}, bf16[160,256]{1,0:T(8,128)(2,1)S(1)}, u32[]{:S(2)}, u32[]{:S(2)}) collective-permute-start(bf16[160,256]{1,0:T(8,128)(2,1)S(1)} %pad_maximum_fusion.2), channel_id=1, source_target_pairs={{0,64},{32,96},{64,128},{96,160},{128,192},{160,224},{192,0},{224,... | collective-permute-start | bytes 245768 | tf_op jit(solution)/shard_map/ppermute | solution.py:27
  20.6 5.5 %collective-permute-start.5 = (bf16[160,256]{1,0:T(8,128)(2,1)S(1)}, bf16[160,256]{1,0:T(8,128)(2,1)S(1)}, u32[]{:S(2)}, u32[]{:S(2)}) collective-permute-start(bf16[160,256]{1,0:T(8,128)(2,1)S(1)} %pad_maximum_fusion.2), channel_id=1, source_target_pairs={{0,224},{32,0},{64,32},{96,64},{128,96},{160,128},{192,160},{224,1... | collective-permute-start | bytes 245768 | tf_op jit(solution)/shard_map/ppermute | solution.py:27
  20.9 5.9 %collective-permute-start.4 = (bf16[160,256]{1,0:T(8,128)(2,1)S(1)}, bf16[160,256]{1,0:T(8,128)(2,1)S(1)}, u32[]{:S(2)}, u32[]{:S(2)}) collective-permute-start(bf16[160,256]{1,0:T(8,128)(2,1)S(1)} %pad_maximum_fusion.2), channel_id=1, source_target_pairs={{0,32},{32,64},{64,96},{96,128},{128,160},{160,192},{192,224},{224... | collective-permute-start | bytes 245768 | tf_op jit(solution)/shard_map/ppermute | solution.py:27
  27.5 20.6 %all-to-all-start = ((s32[64,1,16]{2,1,0:T(1,128)}), s32[64,1,16]{2,1,0:T(1,128)S(1)}, u32[]{:S(2)}, u32[]{:S(2)}) async-start(s32[64,1,16]{2,1,0:T(1,128)} %bitcast.5), calls=%async_computation | async-start | bytes 65536 | tf_op jit(solution)/shard_map/all_to_all | solution.py:22
  49.7 58.7 %copy-start.1 = (f32[1024]{0:T(1024)S(1)}, f32[1024]{0:T(1024)}, u32[]{:S(2)}) copy-start(f32[1024]{0:T(1024)} %param.22) | copy-start | bytes 12292
  49.7 58.7 %copy-start.2 = (f32[8]{0:T(128)S(1)}, f32[8]{0:T(128)}, u32[]{:S(2)}) copy-start(f32[8]{0:T(128)} %bias_ref.1) | copy-start | bytes 100
  49.7 15.3 %all-to-all-start.1 = ((s32[64,1,384]{2,1,0:T(1,128)}), s32[64,1,384]{2,1,0:T(1,128)S(1)}, u32[]{:S(2)}, u32[]{:S(2)}) async-start(s32[64,1,384]{2,1,0:T(1,128)} %copy.27), calls=%async_computation.1 | async-start | bytes 196608 | tf_op jit(solution)/shard_map/all_to_all | solution.py:22
  79.2 29.2 %all-to-all-start.2 = ((bf16[4,512,256]{2,1,0:T(8,128)(2,1)}), bf16[4,512,256]{2,1,0:T(8,128)(2,1)S(1)}, u32[]{:S(2)}, u32[]{:S(2)}) async-start(bf16[4,512,256]{2,1,0:T(8,128)(2,1)} %bitcast.11), calls=%async_computation.2 | async-start | bytes 2097152 | tf_op jit(solution)/shard_map/all_to_all | solution.py:22
  83.5 21.0 %collective-permute-start.3 = (bf16[128,512]{1,0:T(8,128)(2,1)S(1)}, bf16[128,512]{1,0:T(8,128)(2,1)S(1)}, u32[]{:S(2)}, u32[]{:S(2)}) collective-permute-start(bf16[128,512]{1,0:T(8,128)(2,1)S(1)} %get-tuple-element.14), channel_id=1, source_target_pairs={{0,3},{1,0},{2,1},{3,2},{4,7},{5,4},{6,5},{7,6},{8,11},{9,8},{10,9... | collective-permute-start | bytes 393224 | tf_op jit(solution)/shard_map/ppermute | solution.py:27
  86.8 19.2 %collective-permute-start.2 = (bf16[128,512]{1,0:T(8,128)(2,1)S(1)}, bf16[128,512]{1,0:T(8,128)(2,1)S(1)}, u32[]{:S(2)}, u32[]{:S(2)}) collective-permute-start(bf16[128,512]{1,0:T(8,128)(2,1)S(1)} %get-tuple-element.15), channel_id=1, source_target_pairs={{0,2},{1,3},{2,0},{3,1},{4,6},{5,7},{6,4},{7,5},{8,10},{9,11},{10,... | collective-permute-start | bytes 393224 | tf_op jit(solution)/shard_map/ppermute | solution.py:27
  87.7 20.5 %collective-permute-start.1 = (bf16[128,512]{1,0:T(8,128)(2,1)S(1)}, bf16[128,512]{1,0:T(8,128)(2,1)S(1)}, u32[]{:S(2)}, u32[]{:S(2)}) collective-permute-start(bf16[128,512]{1,0:T(8,128)(2,1)S(1)} %get-tuple-element.16), channel_id=1, source_target_pairs={{0,1},{1,2},{2,3},{3,0},{4,5},{5,6},{6,7},{7,4},{8,9},{9,10},{10,1... | collective-permute-start | bytes 393224 | tf_op jit(solution)/shard_map/ppermute | solution.py:27
  108.4 37.9 %copy-start.5 = (s32[8]{0:T(128)S(1)}, s32[8]{0:T(128)}, u32[]{:S(2)}) copy-start(s32[8]{0:T(128)} %param.19) | copy-start | bytes 100
  125.6 18.8 %all-to-all-start.3 = ((bf16[4,512,256]{2,1,0:T(8,128)(2,1)}), bf16[4,512,256]{2,1,0:T(8,128)(2,1)S(1)}, u32[]{:S(2)}, u32[]{:S(2)}) async-start(bf16[4,512,256]{2,1,0:T(8,128)(2,1)} %encoder.1), calls=%async_computation.3 | async-start | bytes 2097152 | tf_op jit(solution)/shard_map/all_to_all | solution.py:22
  144.4 8.4 %copy-start.3 = (bf16[4,512,256]{2,1,0:T(8,128)(2,1)}, bf16[4,512,256]{2,1,0:T(8,128)(2,1)S(1)}, u32[]{:S(2)}) copy-start(bf16[4,512,256]{2,1,0:T(8,128)(2,1)S(1)} %all-to-all-done.3) | copy-start | bytes 3145732
  144.4 8.4 %collective-permute-start.7 = (bf16[256,256]{1,0:T(8,128)(2,1)S(1)}, bf16[256,256]{1,0:T(8,128)(2,1)S(1)}, u32[]{:S(2)}, u32[]{:S(2)}) collective-permute-start(bf16[256,256]{1,0:T(8,128)(2,1)S(1)} %slice.35), channel_id=1, source_target_pairs={{0,4},{4,8},{8,12},{12,16},{16,20},{20,24},{24,28},{28,32},{32,36}... | collective-permute-start | bytes 393224 | tf_op jit(solution)/shard_map/ppermute | solution.py:351
  152.8 0.7 copy-start.4
Sparse Core Ops, SparseCore 0:
  27.7 69.1 all-gather.2
